TPU v7x, 32 devices: a whole 2x2x4 slice. The times are simulated.
32 devices in a mesh: grp: 4 (over y, x), en: 8 (over z, core).
Axes of the slice: x: 2, y: 2, z: 4, core: 2. Of those that a mesh axis runs over, the one named last changes fastest.
Arguments:
- lesser: float32 [2, 512, 4096], P(None, 'grp', 'en'), may hold values from -6 to 6
- greater: float32 [2, 512, 4096], P(None, 'grp', 'en'), may hold values from -6 to 6
- mirror: int32 [512], P('grp'), may hold values from 0 to 511, as said below
Outputs:
- polar: float32 [2, 512, 4096], P(None, 'grp', 'en')
Inputs may be any that keep to these rules, and one draw needn't show every extreme that they name: mirror is an involution without fixed points; for every entry p, mirror[p] // 16 = (p // 16 + 512 // 32) mod (32), so the mirrored entry lies in the aligned block of 16 entries 512 / 2 entries away.
All inputs are finite; a program needn't handle non-finite values.
Results may differ from a plain program's by a relative error of at most 0.000098.
Values sent between devices are 32-bit elements; how exact they have to be, the bound alone decides.
No kernel may reach another device: no remote copies, remote signals or barrier semaphores. Data moves between devices by JAX's collectives and lax.ppermute only.
A program may use at most 64 MiB of HBM per device.

v0:
```python
import math

import jax
import jax.numpy as jnp
from jax import lax
from jax.sharding import PartitionSpec as P


def from_partner(block, axis, distance):
    count = lax.axis_size(axis)
    route = []
    for low in range(count):
        high = low | 1 << distance
        if high != low and high < count:
            route += [(low, high), (high, low)]
    return lax.ppermute(block, axis, route)


def tables(length, sign):
    series = jnp.arange(length, dtype=jnp.int32)
    angle = (
        2.0 * math.pi / length * (series[:, None] * series[None, :] % length).astype(jnp.float32)
    )
    return (jnp.cos(angle), sign * jnp.sin(angle))


def contract(form, left, right):
    return jnp.einsum(form, left, right, precision=lax.Precision.HIGHEST)


def transform(part_re, part_im, sign):
    entries, length = part_re.shape
    radix_high = 128
    radix_low = length // radix_high
    view_re = part_re.reshape(entries, radix_high, radix_low)
    view_im = part_im.reshape(entries, radix_high, radix_low)
    high_re, high_im = tables(radix_high, sign)
    first_re = contract("enm,nk->emk", view_re, high_re) - contract("enm,nk->emk", view_im, high_im)
    first_im = contract("enm,nk->emk", view_re, high_im) + contract("enm,nk->emk", view_im, high_re)
    low_series = jnp.arange(radix_low, dtype=jnp.int32)
    high_series = jnp.arange(radix_high, dtype=jnp.int32)
    twist = (
        2.0
        * math.pi
        / length
        * (low_series[:, None] * high_series[None, :] % length).astype(jnp.float32)
    )
    twist_re = jnp.cos(twist)
    twist_im = sign * jnp.sin(twist)
    turned_re = first_re * twist_re - first_im * twist_im
    turned_im = first_re * twist_im + first_im * twist_re
    low_re, low_im = tables(radix_low, sign)
    final_re = contract("emk,mj->ejk", turned_re, low_re) - contract(
        "emk,mj->ejk", turned_im, low_im
    )
    final_im = contract("emk,mj->ejk", turned_re, low_im) + contract(
        "emk,mj->ejk", turned_im, low_re
    )
    return (final_re.reshape(entries, length), final_im.reshape(entries, length))


def spectra(pieces):
    lesser_part, greater_part = pieces
    fwd_re, fwd_im = transform(lesser_part[0, 0], lesser_part[1, 0], -1.0)
    back_re, back_im = transform(greater_part[0, 0], greater_part[1, 0], 1.0)
    return (jnp.stack([fwd_re, fwd_im])[:, None], jnp.stack([back_re, back_im])[:, None])


def correlate(spec_lesser, spec_greater):
    left_re, left_im = (spec_lesser[0, 0], spec_lesser[1, 0])
    right_re, right_im = (spec_greater[0, 0], spec_greater[1, 0])
    prod_re = left_re * right_re - left_im * right_im
    prod_im = left_re * right_im + left_im * right_re
    length = prod_re.shape[1]
    corr_re, corr_im = transform(prod_re, prod_im, 1.0)
    factor = length ** (-1.5)
    return jnp.stack([corr_im * factor, -corr_re * factor])[:, None]


def body(lesser, greater, mirror):
    group_rows = lesser.shape[1]
    local_len = lesser.shape[2]
    en_count = lax.axis_size("en")
    entry_rows = group_rows // en_count
    top_bit = lax.axis_size("grp").bit_length() - 2
    lesser_view = lesser.reshape(2, en_count, entry_rows, local_len)
    distant = from_partner(greater, "grp", top_bit)
    paired = jnp.take(distant, mirror % group_rows, axis=1)
    paired_view = paired.reshape(2, en_count, entry_rows, local_len)
    spec_lesser, spec_greater = spectra(
        (
            lax.all_to_all(lesser_view, "en", split_axis=1, concat_axis=3, tiled=True),
            lax.all_to_all(paired_view, "en", split_axis=1, concat_axis=3, tiled=True),
        )
    )
    result = correlate(spec_lesser, spec_greater)
    returned = lax.all_to_all(result, "en", split_axis=3, concat_axis=1, tiled=True)
    return returned.reshape(2, group_rows, local_len)


def solution(mesh):
    in_specs = (P(None, "grp", "en"), P(None, "grp", "en"), P("grp"))
    out_specs = P(None, "grp", "en")
    return jax.shard_map(body, mesh=mesh, in_specs=in_specs, out_specs=out_specs, check_vma=False)
```

profile of v0, /device:TPU:0, one launch (start us, length us, event | category | flops | bytes accessed | tf_op | source)
XLA Modules:
  0.0 116.9 jit_solution(292434754670713626)
XLA Ops:
  0.0 1.9 %copy.69 = f32[2,8,16,512]{3,2,0,1:T(8,128)} copy(f32[2,8,16,512]{3,2,1,0:T(8,128)} %bitcast.138) | data formatting | bytes 1048576 | tf_op jit(solution)/shard_map/reshape | solution.py:86
  1.9 6.4 %all-to-all-start = ((f32[2,8,16,512]{3,2,0,1:T(8,128)}), f32[2,8,16,512]{3,2,0,1:T(8,128)S(1)}, u32[]{:S(2)}, u32[]{:S(2)}) async-start(f32[2,8,16,512]{3,2,0,1:T(8,128)} %copy.69), calls=%async_computation | async-start | bytes 1048576 | tf_op jit(solution)/shard_map/all_to_all | solution.py:92
  8.2 1.4 %copy.76 = f32[2,128,512]{2,0,1:T(2,128)S(1)} copy(f32[2,128,512]{2,1,0:T(8,128)} %param.4) | data formatting | bytes 1048576 | tf_op args[1]
  9.7 1.6 %collective-permute-start = (f32[2,128,512]{2,0,1:T(2,128)S(1)}, f32[2,128,512]{2,0,1:T(2,128)S(1)}, u32[]{:S(2)}, u32[]{:S(2)}) collective-permute-start(f32[2,128,512]{2,0,1:T(2,128)S(1)} %copy.76), channel_id=1, source_target_pairs={{0,16},{16,0},{8,24},{24,8},{1,17},{17,1},{9,25},{25,9},{2,18},{18... | collective-permute-start | bytes 1572872 | tf_op jit(solution)/shard_map/ppermute | solution.py:16
  11.3 0.7 compare_and_fusion
  11.9 0.1 broadcast_in_dim.16
  12.0 0.1 fusion.81
  12.1 0.1 broadcast_multiply_fusion
  12.2 11.9 %collective-permute-done = f32[2,128,512]{2,0,1:T(2,128)S(1)} collective-permute-done((f32[2,128,512]{2,0,1:T(2,128)S(1)}, f32[2,128,512]{2,0,1:T(2,128)S(1)}, u32[]{:S(2)}, u32[]{:S(2)}) %collective-permute-start) | collective-permute-done | bytes 524320 | tf_op jit(solution)/shard_map/ppermute | solution.py:16
  24.1 1.1 gather_fusion
  25.2 1.0 copy_select_fusion
  26.2 0.0 all-to-all-done
  26.2 4.7 %all-to-all-start.1 = ((f32[2,8,16,512]{3,2,0,1:T(8,128)}), f32[2,8,16,512]{3,2,0,1:T(8,128)S(1)}, u32[]{:S(2)}, u32[]{:S(2)}) async-start(f32[2,8,16,512]{3,2,0,1:T(8,128)} %copy_select_fusion), calls=%async_computation.1 | async-start | bytes 1048576 | tf_op jit(solution)/shard_map/all_to_all | solution.py:93
  31.0 0.2 copy.72
  31.1 0.3 reshape_squeeze.13
  31.4 0.3 copy.73
  31.7 0.6 fusion.31
  32.3 0.6 fusion.41
  33.0 0.2 copy.70
  33.1 0.3 reshape_squeeze.12
  33.4 0.3 copy.71
  33.7 0.6 fusion.29
  34.4 0.6 fusion.43
  35.0 0.1 fusion.6
  35.1 0.4 fusion.57
  35.6 0.4 fusion.65
  36.0 0.4 convolution_add_fusion.2
  36.5 9.8 %all-to-all-done.1 = f32[2,8,16,512]{3,2,0,1:T(8,128)S(1)} async-done(((f32[2,8,16,512]{3,2,0,1:T(8,128)}), f32[2,8,16,512]{3,2,0,1:T(8,128)S(1)}, u32[]{:S(2)}, u32[]{:S(2)}) %all-to-all-start.1) | async-done | bytes 524320 | tf_op jit(solution)/shard_map/all_to_all | solution.py:93
  46.3 0.2 copy.78
  46.4 0.3 reshape_squeeze.14
  46.7 1.8 %fusion.17 = f32[16,32,128]{2,1,0:T(8,128)S(1)} fusion(f32[16,128,32]{2,1,0:T(8,128)S(1)} %reshape_squeeze.14), kind=kOutput, calls=%fused_computation.43 | convolution fusion | flops 100892672 | bytes 524288 | tf_op jit(solution)/shard_map/enm,nk->emk/dot_general | solution.py:28
  48.5 1.8 %fusion.24 = f32[16,32,128]{2,1,0:T(8,128)S(1)} fusion(f32[16,128,32]{2,1,0:T(8,128)S(1)} %reshape_squeeze.14), kind=kOutput, calls=%fused_computation.50 | convolution fusion | flops 100892672 | bytes 524288 | tf_op jit(solution)/shard_map/enm,nk->emk/dot_general | solution.py:28
  50.3 0.2 copy.80
  50.5 0.3 reshape_squeeze.15
  50.7 1.8 %convolution_add_fusion.4 = f32[16,32,128]{2,1,0:T(8,128)S(1)} fusion(f32[16,32,128]{2,1,0:T(8,128)S(1)} %fusion.17, f32[16,128,32]{2,1,0:T(8,128)S(1)} %reshape_squeeze.15), kind=kOutput, calls=%fused_computation.14 | convolution fusion | flops 100958208 | bytes 786432 | tf_op jit(solution)/shard_map/enm,nk->emk/dot_general | solution.py:28
  52.5 1.8 %convolution_subtract_fusion.4 = f32[16,32,128]{2,1,0:T(8,128)S(1)} fusion(f32[16,32,128]{2,1,0:T(8,128)S(1)} %fusion.24, f32[16,128,32]{2,1,0:T(8,128)S(1)} %reshape_squeeze.15), kind=kOutput, calls=%fused_computation.15 | convolution fusion | flops 100958208 | bytes 786432 | tf_op jit(solution)/shard_map/enm,nk->emk/dot_general | solution.py:28
  54.3 0.5 fusion.7
  54.8 0.7 fusion.8
  55.4 0.5 convolution_add_fusion.1
  55.9 0.5 convolution_subtract_fusion.1
  56.4 0.5 add_bitcast_fusion
  56.9 0.3 sub.52
  57.2 1.8 %fusion.21 = f32[16,32,128]{2,1,0:T(8,128)S(1)} fusion(f32[16,128,32]{2,1,0:T(8,128)S(1)} %sub.52), kind=kOutput, calls=%fused_computation.47 | convolution fusion | flops 100892672 | bytes 524288 | tf_op jit(solution)/shard_map/enm,nk->emk/dot_general | solution.py:28
  59.0 1.8 %fusion.14 = f32[16,32,128]{2,1,0:T(8,128)S(1)} fusion(f32[16,128,32]{2,1,0:T(8,128)S(1)} %sub.52), kind=kOutput, calls=%fused_computation.40 | convolution fusion | flops 100892672 | bytes 524288 | tf_op jit(solution)/shard_map/enm,nk->emk/dot_general | solution.py:28
  60.7 0.3 add.175
  61.0 1.8 %convolution_subtract_fusion.3 = f32[16,32,128]{2,1,0:T(8,128)S(1)} fusion(f32[16,32,128]{2,1,0:T(8,128)S(1)} %fusion.21, f32[16,128,32]{2,1,0:T(8,128)S(1)} %add.175), kind=kOutput, calls=%fused_computation.13 | convolution fusion | flops 100958208 | bytes 786432 | tf_op jit(solution)/shard_map/enm,nk->emk/dot_general | solution.py:28
  62.8 1.8 %convolution_add_fusion.3 = f32[16,32,128]{2,1,0:T(8,128)S(1)} fusion(f32[16,32,128]{2,1,0:T(8,128)S(1)} %fusion.14, f32[16,128,32]{2,1,0:T(8,128)S(1)} %add.175), kind=kOutput, calls=%fused_computation.12 | convolution fusion | flops 100958208 | bytes 786432 | tf_op jit(solution)/shard_map/enm,nk->emk/dot_general | solution.py:28
  64.6 0.5 fusion.10
  65.0 0.5 fusion.9
  65.5 0.5 fusion.4
  66.0 0.1 mul.599
  66.0 0.5 fusion.2
  66.5 0.1 mul.602
  66.6 4.4 %copy.88 = f32[2,16,4096]{1,0,2:T(2,128)} copy(f32[2,16,4096]{2,1,0:T(8,128)S(1)} %pad_maximum_fusion) | data formatting | bytes 1048576 | tf_op jit(solution)/shard_map/stack | solution.py:77
  71.0 4.7 %bitcast_bitcast_fusion = f32[4096,1,2,16]{3,2,1,0:T(2,128)} fusion(f32[2,16,4096]{1,0,2:T(2,128)} %copy.88), kind=kLoop, calls=%fused_computation.215 | loop fusion | bytes 1048576
  75.7 7.2 %reshape.152 = f32[8,1,16384]{2,1,0:T(1,128)S(1)} reshape(f32[4096,1,2,16]{3,2,1,0:T(2,128)} %bitcast_bitcast_fusion) | data formatting | bytes 1048576
  82.9 17.7 %all_to_all.45 = f32[8,1,16384]{2,1,0:T(1,128)S(1)} all-to-all(f32[8,1,16384]{2,1,0:T(1,128)S(1)} %reshape.152), channel_id=1, replica_groups=mesh['grp'=4,'en'=8] {'en'}, dimensions={0} | all-to-all | bytes 1048576 | tf_op jit(solution)/shard_map/all_to_all | solution.py:97
  100.7 0.5 broadcast.335
  101.2 1.9 %reduce = f32[8,16384]{1,0:T(8,128)S(1)} reduce(f32[8,1,16384]{2,1,0:T(1,128)S(1)} %all_to_all.45, f32[]{:T(128)} %broadcast.335), dimensions={1}, to_apply=%all_to_all.39.reduce_sub_computation | reduce | bytes 1048580 | tf_op jit(solution)/shard_map/all_to_all | solution.py:97
  103.1 7.5 %reshape.153 = f32[4096,1,2,16]{3,2,1,0:T(2,128)} reshape(f32[8,16384]{1,0:T(8,128)S(1)} %reduce) | data formatting | bytes 1048576
  110.6 6.3 %copy.89 = f32[2,8,1,16,512]{4,3,1,0,2:T(8,128)} copy(f32[2,8,1,16,512]{3,0,4,1,2:T(2,128)} %bitcast.126) | data formatting | bytes 1048576 | tf_op jit(solution)/shard_map/all_to_all | solution.py:97
  (4 shorter events, 0.1 us)
Async XLA Ops:
  1.9 24.3 %all-to-all-start = ((f32[2,8,16,512]{3,2,0,1:T(8,128)}), f32[2,8,16,512]{3,2,0,1:T(8,128)S(1)}, u32[]{:S(2)}, u32[]{:S(2)}) async-start(f32[2,8,16,512]{3,2,0,1:T(8,128)} %copy.69), calls=%async_computation | async-start | bytes 1048576 | tf_op jit(solution)/shard_map/all_to_all | solution.py:92
  9.7 14.4 %collective-permute-start = (f32[2,128,512]{2,0,1:T(2,128)S(1)}, f32[2,128,512]{2,0,1:T(2,128)S(1)}, u32[]{:S(2)}, u32[]{:S(2)}) collective-permute-start(f32[2,128,512]{2,0,1:T(2,128)S(1)} %copy.76), channel_id=1, source_target_pairs={{0,16},{16,0},{8,24},{24,8},{1,17},{17,1},{9,25},{25,9},{2,18},{18... | collective-permute-start | bytes 1572872 | tf_op jit(solution)/shard_map/ppermute | solution.py:16
  26.2 20.0 %all-to-all-start.1 = ((f32[2,8,16,512]{3,2,0,1:T(8,128)}), f32[2,8,16,512]{3,2,0,1:T(8,128)S(1)}, u32[]{:S(2)}, u32[]{:S(2)}) async-start(f32[2,8,16,512]{3,2,0,1:T(8,128)} %copy_select_fusion), calls=%async_computation.1 | async-start | bytes 1048576 | tf_op jit(solution)/shard_map/all_to_all | solution.py:93
where the time goes:
time: 118 us; the launch traced here: 117 us
  local copies, waits for them, and re-layouts  38.2 us (32%)
  matrix products  22.5 us (19%)
  waiting for transfers between devices  21.7 us (18%)
  blocking collectives  17.7 us (15%)
  starting transfers between devices  12.6 us (11%)
  other arithmetic  3.85 us (3%)
    unnamed x4, local copies, waits for them, and re-layouts  20.9 us
    dot_general x20, matrix products, contract(): return jnp.einsum(form, left, right, precision=lax.Precision.HIGHEST)  19.9 us
    all_to_all x1, blocking collectives, body(): lax.all_to_all(result, 'en', split_axis=3, concat_axis=1, tiled=True)  17.7 us
    ppermute x1, waiting for transfers between devices, from_partner(): return lax.ppermute(block, axis, route)  11.9 us
    all_to_all x1, waiting for transfers between devices, body(): lax.all_to_all(paired_view, 'en', split_axis=1, concat_axis=3, tiled=True)  9.78 us
    all_to_all x2, local copies, waits for them, and re-layouts, body(): lax.all_to_all(result, 'en', split_axis=3, concat_axis=1, tiled=True)  6.78 us
    all_to_all x1, starting transfers between devices, body(): lax.all_to_all(lesser_view, 'en', split_axis=1, concat_axis=3, tiled=True)  6.35 us
    all_to_all x1, starting transfers between devices, body(): lax.all_to_all(paired_view, 'en', split_axis=1, concat_axis=3, tiled=True)  4.71 us
  transfers between devices with their start and end apart: 3, of which 2 were waited for; matrix products, arithmetic and copies ran while one was open for 8% of the time, Pallas kernels for 0%

commit v1 on v0

v1 whole, which is shorter than its diff:
```python
import functools
import math

import jax
import jax.numpy as jnp
import numpy as np
from jax import lax
from jax.experimental import pallas as pl
from jax.experimental.pallas import tpu as pltpu
from jax.sharding import Mesh
from jax.sharding import PartitionSpec as P

LANES = 128
SUBLANES = 8


def dft_block(scale):
    turn = 2.0 * math.pi / LANES * (np.outer(np.arange(LANES), np.arange(LANES)) % LANES)
    cos, sin = np.cos(turn), np.sin(turn)
    full = (np.block([[cos, -sin], [sin, cos]]) * scale).astype(np.float32)
    high = full.astype(jnp.bfloat16)
    low = (full - high.astype(np.float32)).astype(jnp.bfloat16)
    return np.stack([high, low])


def twiddles(points):
    length = points * LANES
    turn = 2.0 * math.pi / length * (np.outer(np.arange(points), np.arange(LANES)) % length)
    return np.stack([np.cos(turn), -np.sin(turn)]).astype(np.float32)


def times_root(value, numerator, denominator):
    re, im = value
    eighths = 8 * numerator / denominator % 8
    if eighths == 0:
        return re, im
    if eighths == 2:
        return im, -re
    if eighths == 4:
        return -re, -im
    if eighths == 6:
        return -im, re
    half = math.sqrt(0.5)
    if eighths == 1:
        return (re + im) * half, (im - re) * half
    if eighths == 3:
        return (im - re) * half, -(re + im) * half
    turn = 2.0 * math.pi * numerator / denominator
    cos, sin = math.cos(turn), math.sin(turn)
    return re * cos + im * sin, im * cos - re * sin


def add(a, b):
    return a[0] + b[0], a[1] + b[1]


def sub(a, b):
    return a[0] - b[0], a[1] - b[1]


def small_dft(values):
    count = len(values)
    if count == 1:
        return values
    even, odd = small_dft(values[0::2]), small_dft(values[1::2])
    odd = [times_root(v, k, count) for k, v in enumerate(odd)]
    return [add(e, o) for e, o in zip(even, odd)] + [sub(e, o) for e, o in zip(even, odd)]


def long_dft(load, keep, points):
    first = min(8, points)
    second = points // first
    for s in range(second):
        for k, value in enumerate(small_dft([load(e * second + s) for e in range(first)])):
            keep[k * second + s, 0], keep[k * second + s, 1] = times_root(value, s * k, points)
    for k in range(first):
        group = [(keep[k * second + s, 0], keep[k * second + s, 1]) for s in range(second)]
        for j, value in enumerate(small_dft(group)):
            yield k + first * j, value


def split_store(ref, row, rows, re, im):
    for place, part in enumerate((re, im)):
        high = part.astype(jnp.bfloat16)
        low = (part - high.astype(jnp.float32)).astype(jnp.bfloat16)
        ref[0, pl.ds(row, rows), place * LANES : (place + 1) * LANES] = high
        ref[1, pl.ds(row, rows), place * LANES : (place + 1) * LANES] = low


def dot(left, right):
    return jnp.dot(left, right, preferred_element_type=jnp.float32)


def lane_dft(halves, table):
    high, low = halves[0], halves[1]
    return dot(high, table[0]) + dot(low, table[0]) + dot(high, table[1])


def pack_kernel(lesser, greater, packed, sems):
    own = lax.axis_index("half")
    copies = []
    count = packed.shape[0] // 2
    rows = packed.shape[2]
    for which, source in enumerate((lesser, greater)):
        place = jnp.where(own == which, 0, count)
        for part in range(2):
            for e in range(count):
                copies.append(
                    pltpu.make_async_copy(
                        source.at[part, pl.ds(e * rows, rows)],
                        packed.at[place + e, part],
                        sems.at[which, part, e],
                    )
                )
    for copy in copies:
        copy.start()
    for copy in copies:
        copy.wait()


def correlate_kernel(mirror, got, forward, backward, twist, out, keep, halves, left, right):
    count = got.shape[0] // 2
    rows = got.shape[2]
    steps = got.shape[3] // LANES
    points = count * steps
    group_rows = mirror.shape[0]
    own = lax.axis_index("half")
    base = lax.axis_index("en") * rows

    def read(start, swap):
        def load(t):
            where = slice(t % steps * LANES, (t % steps + 1) * LANES)
            re = got[start + t // steps, 0, :, where]
            im = got[start + t // steps, 1, :, where]
            return (im, re) if swap else (re, im)

        return load

    def twisted(k, value):
        re, im = value
        cos, sin = twist[0, pl.ds(k, 1), :], twist[1, pl.ds(k, 1), :]
        return re * cos - im * sin, re * sin + im * cos

    for which, target in enumerate((left, right)):
        start = jnp.where(own == which, 0, count)
        for k, value in long_dft(read(start, which == 1), keep, points):
            split_store(halves, k * rows, rows, *twisted(k, value))
        target[...] = lane_dft(halves, forward)

    line = lax.broadcasted_iota(jnp.int32, (rows, LANES), 0)
    order = jnp.zeros((rows, LANES), jnp.int32)
    for row in range(rows):
        order = jnp.where(line == row, mirror[base + row] % group_rows - base, order)
    tiles = rows // SUBLANES
    inner = order % SUBLANES
    tile = order // SUBLANES

    def permuted(value):
        out_tiles = []
        for to in range(tiles):
            span = slice(to * SUBLANES, (to + 1) * SUBLANES)
            result = jnp.zeros((SUBLANES, LANES), jnp.float32)
            for source in range(tiles):
                block = value[source * SUBLANES : (source + 1) * SUBLANES]
                moved = jnp.take_along_axis(block, inner[span], axis=0)
                result = jnp.where(tile[span] == source, moved, result)
            out_tiles.append(result)
        return jnp.concatenate(out_tiles, axis=0)

    for k in range(points):
        span = pl.ds(k * rows, rows)
        a_re, a_im = left[span, :LANES], left[span, LANES:]
        b_im, b_re = permuted(right[span, :LANES]), permuted(right[span, LANES:])
        split_store(halves, k * rows, rows, a_re * b_im + a_im * b_re, a_re * b_re - a_im * b_im)
    left[...] = lane_dft(halves, backward)

    def spectrum(k):
        return twisted(k, (left[pl.ds(k * rows, rows), :LANES], left[pl.ds(k * rows, rows), LANES:]))

    for t, (c_im, c_re) in long_dft(spectrum, keep, points):
        where = slice(t % steps * LANES, (t % steps + 1) * LANES)
        out[t // steps, 0, :, where] = c_im
        out[t // steps, 1, :, where] = -c_re


def body(lesser, greater, mirror):
    _, group_rows, local_len = lesser.shape
    count = lax.axis_size("en")
    rows = group_rows // count
    length = local_len * count
    points = length // LANES
    block = (2, rows, local_len)
    in_vmem = pl.BlockSpec(memory_space=pltpu.VMEM)
    in_place = pl.BlockSpec(memory_space=pl.ANY)

    packed = pl.pallas_call(
        pack_kernel,
        out_shape=jax.ShapeDtypeStruct((2 * count, *block), jnp.float32),
        in_specs=[in_place, in_place],
        out_specs=in_vmem,
        scratch_shapes=[pltpu.SemaphoreType.DMA((2, 2, count))],
        compiler_params=pltpu.CompilerParams(vmem_limit_bytes=8 << 20),
    )(lesser, greater)
    got = lax.all_to_all(packed, ("half", "en"), 0, 0, tiled=True)
    result = pl.pallas_call(
        correlate_kernel,
        out_shape=jax.ShapeDtypeStruct((count, *block), jnp.float32),
        in_specs=[pl.BlockSpec(memory_space=pltpu.SMEM)] + [in_vmem] * 4,
        out_specs=in_vmem,
        scratch_shapes=[
            pltpu.VMEM((points, 2, rows, LANES), jnp.float32),
            pltpu.VMEM((2, points * rows, 2 * LANES), jnp.bfloat16),
            pltpu.VMEM((points * rows, 2 * LANES), jnp.float32),
            pltpu.VMEM((points * rows, 2 * LANES), jnp.float32),
        ],
        compiler_params=pltpu.CompilerParams(vmem_limit_bytes=24 << 20),
    )(
        mirror,
        got,
        jnp.asarray(dft_block(1.0)),
        jnp.asarray(dft_block(length**-1.5)),
        jnp.asarray(twiddles(points)),
    )
    returned = lax.all_to_all(result, "en", 0, 0, tiled=True)
    return jnp.transpose(returned, (1, 0, 2, 3)).reshape(2, group_rows, local_len)


def solution(mesh):
    groups = mesh.shape["grp"]
    devices = mesh.devices.reshape(2, groups // 2, mesh.shape["en"])
    finer = Mesh(devices, ("half", "grp", "en"))
    spec = P(None, ("half", "grp"), "en")
    in_specs = (spec, spec, P(("half", "grp")))
    return jax.shard_map(body, mesh=finer, in_specs=in_specs, out_specs=spec, check_vma=False)
```

time: 118 us -> 59.3 us (0.50)
  local copies, waits for them, and re-layouts: 38.2 us -> 2.95 us
  blocking collectives: 17.7 us -> 51.8 us
  matrix products: 22.5 us -> 0 us
  waiting for transfers between devices: 21.7 us -> 0 us
  starting transfers between devices: 12.6 us -> 0 us
  Pallas kernels: 0 us -> 4.17 us
  other arithmetic: 3.85 us -> 0 us
    all_to_all x1 -> x2, blocking collectives: 17.7 us -> 51.8 us  [the longest x1 32.5 us: body(): got = lax.all_to_all(packed, ('half', 'en'), 0, 0, tiled=True)]
    dot_general x20 -> x0, matrix products: 19.9 us -> none  [contract(): return jnp.einsum(form, left, right, precision=lax.Precision.HIGHEST)]
    unnamed x4 -> x12, local copies, waits for them, and re-layouts: 20.9 us -> 2.11 us
    ppermute x1 -> x0, waiting for transfers between devices: 11.9 us -> none  [from_partner(): return lax.ppermute(block, axis, route)]
    all_to_all x2 -> x0, starting transfers between devices: 11.1 us -> none  [the longest x1 6.35 us: body(): lax.all_to_all(lesser_view, 'en', split_axis=1, concat_axis=3, tiled=True)]
    all_to_all x2 -> x0, waiting for transfers between devices: 9.78 us -> none  [the longest x1 9.78 us: body(): lax.all_to_all(paired_view, 'en', split_axis=1, concat_axis=3, tiled=True)]
    all_to_all x2 -> x0, local copies, waits for them, and re-layouts: 6.78 us -> none  [body(): lax.all_to_all(result, 'en', split_axis=3, concat_axis=1, tiled=True)]
    another operation x7 -> x0, local copies, waits for them, and re-layouts: 6.08 us -> none  [the longest x1 4.38 us: correlate(): return jnp.stack([corr_im * factor, -corr_re * factor])[:, None]]
  transfers between devices with their start and end apart: 3 -> 0, of which waited for: 2 -> 0; matrix products, arithmetic and copies ran while one was open for 8% -> 0% of each run, Pallas kernels for 0% -> 0%
where the time goes in v1:
time: 59.3 us; the launch traced here: 59 us
  blocking collectives  51.8 us (87%)
  Pallas kernels  4.17 us (7%)
  local copies, waits for them, and re-layouts  2.95 us (5%)
    all_to_all x1, blocking collectives, body(): got = lax.all_to_all(packed, ('half', 'en'), 0, 0, tiled=True)  32.5 us
    all_to_all x1, blocking collectives, body(): returned = lax.all_to_all(result, 'en', 0, 0, tiled=True)  19.3 us
    pallas_call x1, Pallas kernels, body(): pl.pallas_call(correlate_kernel, out_shape=jax.ShapeDtypeStruct((count, *...  2.5 us
    unnamed x12, local copies, waits for them, and re-layouts  2.11 us
    pallas_call x1, Pallas kernels, body(): pl.pallas_call(pack_kernel, out_shape=jax.ShapeDtypeStruct((2 * count, *b...  1.67 us

profile of v1, /device:TPU:0, one launch (start us, length us, event | category | flops | bytes accessed | tf_op | source)
XLA Modules:
  0.0 59.0 jit_solution(9034290333357887636)
XLA Ops:
  0.0 0.0 copy-start
  0.0 1.0 %copy-done = f32[2,128,512]{2,1,0:T(8,128)S(1)} copy-done((f32[2,128,512]{2,1,0:T(8,128)S(1)}, f32[2,128,512]{2,1,0:T(8,128)}, u32[]{:S(2)}) %copy-start) | copy-done | bytes 524312
  1.0 0.0 copy-start.1
  1.0 1.0 %copy-done.1 = f32[2,128,512]{2,1,0:T(8,128)S(1)} copy-done((f32[2,128,512]{2,1,0:T(8,128)S(1)}, f32[2,128,512]{2,1,0:T(8,128)}, u32[]{:S(2)}) %copy-start.1) | copy-done | bytes 524312
  2.1 1.7 %shard_map.64 = f32[16,2,16,512]{3,2,1,0:T(8,128)S(1)} custom-call(f32[2,128,512]{2,1,0:T(8,128)S(1)} %copy-done, f32[2,128,512]{2,1,0:T(8,128)S(1)} %copy-done.1), custom_call_target="tpu_custom_call" | custom-call | tf_op jit(solution)/shard_map/pallas_call | solution.py:196
  3.8 0.0 copy-start.2
  3.8 0.0 copy-start.3
  3.8 0.0 copy-start.4
  3.8 0.0 copy-start.5
  3.8 32.5 %all_to_all.10.got = f32[16,2,16,512]{3,2,1,0:T(8,128)S(1)} all-to-all(f32[16,2,16,512]{3,2,1,0:T(8,128)S(1)} %shard_map.64), channel_id=1, replica_groups=mesh['half'=2,'grp'=2,'en'=8] {'half','en'}, dimensions={0} | all-to-all | bytes 2097152 | tf_op jit(solution)/shard_map/all_to_all | solution.py:204
  36.3 0.0 copy-done.2
  36.3 0.0 copy-done.3
  36.3 0.0 copy-done.4
  36.4 0.0 copy-done.5
  36.4 2.5 %shard_map.65 = f32[8,2,16,512]{3,2,1,0:T(8,128)S(1)} custom-call(s32[128]{0:T(128)S(1)} %copy-done.5, f32[16,2,16,512]{3,2,1,0:T(8,128)S(1)} %all_to_all.10.got, bf16[2,256,256]{2,1,0:T(8,128)(2,1)S(1)} %copy-done.3, bf16[2,256,256]{2,1,0:T(8,128)(2,1)S(1)} %copy-done.2, f32[2,32,128]{2,1,0:T(8,128)S(1)} %copy-done.4), custom_call_target="tpu_custom_call" | custom-call | tf_op jit(solution)/shard_map/pallas_call | solution.py:205
  38.9 19.3 %all_to_all.11 = f32[8,2,16,512]{3,2,1,0:T(8,128)S(1)} all-to-all(f32[8,2,16,512]{3,2,1,0:T(8,128)S(1)} %shard_map.65), channel_id=1, replica_groups=mesh['half'=2,'grp'=2,'en'=8] {'en'}, dimensions={0} | all-to-all | bytes 1048576 | tf_op jit(solution)/shard_map/all_to_all | solution.py:224
  58.2 0.8 %copy.7 = f32[2,8,16,512]{3,2,1,0:T(8,128)} copy(f32[2,8,16,512]{3,2,0,1:T(8,128)S(1)} %bitcast.2) | data formatting | bytes 1048576 | tf_op jit(solution)/shard_map/transpose | solution.py:225
Async XLA Ops:
  0.0 1.0 %copy-start = (f32[2,128,512]{2,1,0:T(8,128)S(1)}, f32[2,128,512]{2,1,0:T(8,128)}, u32[]{:S(2)}) copy-start(f32[2,128,512]{2,1,0:T(8,128)} %lesser.1) | copy-start | bytes 1572868
  1.0 1.0 %copy-start.1 = (f32[2,128,512]{2,1,0:T(8,128)S(1)}, f32[2,128,512]{2,1,0:T(8,128)}, u32[]{:S(2)}) copy-start(f32[2,128,512]{2,1,0:T(8,128)} %greater.1) | copy-start | bytes 1572868
  3.8 32.6 %copy-start.2 = (bf16[2,256,256]{2,1,0:T(8,128)(2,1)S(1)}, bf16[2,256,256]{2,1,0:T(8,128)(2,1)}, u32[]{:S(2)}) copy-start(bf16[2,256,256]{2,1,0:T(8,128)(2,1)} %constant.7.clone.backward) | copy-start | bytes 786436
  3.8 32.6 %copy-start.3 = (bf16[2,256,256]{2,1,0:T(8,128)(2,1)S(1)}, bf16[2,256,256]{2,1,0:T(8,128)(2,1)}, u32[]{:S(2)}) copy-start(bf16[2,256,256]{2,1,0:T(8,128)(2,1)} %constant.6.clone.forward) | copy-start | bytes 786436
  3.8 32.6 %copy-start.4 = (f32[2,32,128]{2,1,0:T(8,128)S(1)}, f32[2,32,128]{2,1,0:T(8,128)}, u32[]{:S(2)}) copy-start(f32[2,32,128]{2,1,0:T(8,128)} %constant.8.clone.twist) | copy-start | bytes 98308
  3.8 32.6 %copy-start.5 = (s32[128]{0:T(128)S(1)}, s32[128]{0:T(128)}, u32[]{:S(2)}) copy-start(s32[128]{0:T(128)} %mirror.1) | copy-start | bytes 1540

commit v2 on v1

v2 whole, which is shorter than its diff:
```python
import functools
import math

import jax
import jax.numpy as jnp
import numpy as np
from jax import lax
from jax.experimental import pallas as pl
from jax.experimental.pallas import tpu as pltpu
from jax.sharding import Mesh
from jax.sharding import PartitionSpec as P

LANES = 128
SUBLANES = 8


def dft_block(scale):
    turn = 2.0 * math.pi / LANES * (np.outer(np.arange(LANES), np.arange(LANES)) % LANES)
    cos, sin = np.cos(turn), np.sin(turn)
    full = (np.block([[cos, -sin], [sin, cos]]) * scale).astype(np.float32)
    high = full.astype(jnp.bfloat16)
    low = (full - high.astype(np.float32)).astype(jnp.bfloat16)
    return np.stack([high, low])


def twiddles(points):
    length = points * LANES
    turn = 2.0 * math.pi / length * (np.outer(np.arange(points), np.arange(LANES)) % length)
    return np.stack([np.cos(turn), -np.sin(turn)]).astype(np.float32)


def times_root(value, numerator, denominator):
    re, im = value
    eighths = 8 * numerator / denominator % 8
    if eighths == 0:
        return re, im
    if eighths == 2:
        return im, -re
    if eighths == 4:
        return -re, -im
    if eighths == 6:
        return -im, re
    half = math.sqrt(0.5)
    if eighths == 1:
        return (re + im) * half, (im - re) * half
    if eighths == 3:
        return (im - re) * half, -(re + im) * half
    turn = 2.0 * math.pi * numerator / denominator
    cos, sin = math.cos(turn), math.sin(turn)
    return re * cos + im * sin, im * cos - re * sin


def add(a, b):
    return a[0] + b[0], a[1] + b[1]


def sub(a, b):
    return a[0] - b[0], a[1] - b[1]


def small_dft(values):
    count = len(values)
    if count == 1:
        return values
    even, odd = small_dft(values[0::2]), small_dft(values[1::2])
    odd = [times_root(v, k, count) for k, v in enumerate(odd)]
    return [add(e, o) for e, o in zip(even, odd)] + [sub(e, o) for e, o in zip(even, odd)]


def long_dft(load, keep, points):
    first = min(8, points)
    second = points // first
    for s in range(second):
        for k, value in enumerate(small_dft([load(e * second + s) for e in range(first)])):
            keep[k * second + s, 0], keep[k * second + s, 1] = times_root(value, s * k, points)
    for k in range(first):
        group = [(keep[k * second + s, 0], keep[k * second + s, 1]) for s in range(second)]
        for j, value in enumerate(small_dft(group)):
            yield k + first * j, value


def split_store(ref, row, rows, re, im):
    for place, part in enumerate((re, im)):
        high = part.astype(jnp.bfloat16)
        low = (part - high.astype(jnp.float32)).astype(jnp.bfloat16)
        ref[0, pl.ds(row, rows), place * LANES : (place + 1) * LANES] = high
        ref[1, pl.ds(row, rows), place * LANES : (place + 1) * LANES] = low


def dot(left, right):
    return jnp.dot(left, right, preferred_element_type=jnp.float32)


def lane_dft(halves, table):
    high, low = halves[0], halves[1]
    return dot(high, table[0]) + dot(low, table[0]) + dot(high, table[1])


def times_twist(twist, k, value):
    re, im = value
    cos, sin = twist[0, pl.ds(k, 1), :], twist[1, pl.ds(k, 1), :]
    return re * cos - im * sin, re * sin + im * cos


def pack_kernel(mirror, lesser, greater, packed, *rest):
    blocks, (held, block_sems, chunk_sems, held_sems) = rest[:-4], rest[-4:]
    _, count, tiles, sub, local_len = lesser.shape
    rows = tiles * sub
    own = lax.axis_index("half")
    me = lax.axis_index("en")
    loads = [pltpu.make_async_copy(greater.at[p], held.at[p], held_sems.at[p]) for p in range(2)]
    moves = [
        pltpu.make_async_copy(
            lesser.at[p, :, 0], packed.at[pl.ds(own * count, count), p], chunk_sems.at[p]
        )
        for p in range(2)
    ]
    moves += [
        pltpu.make_async_copy(lesser.at[:, me ^ s, 1], blocks[s], block_sems.at[s])
        for s in range(count)
    ]
    for copy in loads + moves:
        copy.start()
    line = lax.broadcasted_iota(jnp.int32, (sub, LANES), 0)
    for copy in loads:
        copy.wait()
    for s in range(count):
        to = me ^ s
        orders = [jnp.zeros((sub, LANES), jnp.int32) for _ in range(tiles)]
        for row in range(rows):
            place = mirror[to * rows + row] % rows
            orders = [jnp.where(line + t * sub == place, row, o) for t, o in enumerate(orders)]
        for part in range(2):
            for lane in range(0, local_len, LANES):
                span = slice(lane, lane + LANES)
                sources = [held[part, to, t, :, span] for t in range(tiles)]
                for t, order in enumerate(orders):
                    moved = jnp.zeros((sub, LANES), jnp.float32)
                    for u, source in enumerate(sources):
                        picked = jnp.take_along_axis(source, order % sub, axis=0)
                        moved = jnp.where(order // sub == u, picked, moved)
                    if t == 0:
                        packed[(1 - own) * count + to, part, :, span] = moved
                    else:
                        blocks[count + s][part, :, span] = moved
    for copy in moves:
        copy.wait()


def correlate(got, forward, backward, twist, out, keep, halves, left, right):
    count = got.shape[0] // 2
    rows = got.shape[2]
    steps = got.shape[3] // LANES
    points = count * steps
    own = lax.axis_index("half")

    def read(start, swap):
        def load(t):
            where = slice(t % steps * LANES, (t % steps + 1) * LANES)
            re = got[start + t // steps, 0, :, where]
            im = got[start + t // steps, 1, :, where]
            return (im, re) if swap else (re, im)

        return load

    for which, target in enumerate((left, right)):
        start = jnp.where(own == which, 0, count)
        for k, value in long_dft(read(start, which == 1), keep, points):
            split_store(halves, k * rows, rows, *times_twist(twist, k, value))
        target[...] = lane_dft(halves, forward)

    for k in range(points):
        span = pl.ds(k * rows, rows)
        a_re, a_im = left[span, :LANES], left[span, LANES:]
        b_im, b_re = right[span, :LANES], right[span, LANES:]
        split_store(halves, k * rows, rows, a_re * b_im + a_im * b_re, a_re * b_re - a_im * b_im)
    left[...] = lane_dft(halves, backward)

    def spectrum(k):
        span = pl.ds(k * rows, rows)
        return times_twist(twist, k, (left[span, :LANES], left[span, LANES:]))

    for t, (c_im, c_re) in long_dft(spectrum, keep, points):
        where = slice(t % steps * LANES, (t % steps + 1) * LANES)
        out[t // steps, 0, :, where] = c_im
        out[t // steps, 1, :, where] = -c_re


def correlate_pieces(pieces, *refs):
    got, blocks, rest = refs[-1], refs[:pieces], refs[pieces:-1]
    count = pieces // 2
    own = lax.axis_index("half")
    me = lax.axis_index("en")
    for s, block in enumerate(blocks):
        half = own if s < count else 1 - own
        got[half * count + (me ^ (s % count))] = block[...]
    correlate(got, *rest)


def hold_kernel(block, out):
    out[...] = block[...]


def far_first(count):
    return sorted(range(1, 2 * count), key=lambda s: (-(s % count // 2), s < count, s))


def unpack_kernel(chunk, *refs):
    returned, out, sems = refs[0], refs[-2], refs[-1]
    copies = [
        pltpu.make_async_copy(returned.at[:, p], out.at[p, :, chunk], sems.at[p]) for p in range(2)
    ]
    for copy in copies:
        copy.start()
    for copy in copies:
        copy.wait()


def body(lesser, greater, mirror):
    _, group_rows, local_len = lesser.shape
    count = lax.axis_size("en")
    rows = group_rows // count
    tiles = rows // SUBLANES
    length = local_len * count
    points = length // LANES
    block = (2, SUBLANES, local_len)
    tiled = (2, count, tiles, SUBLANES, local_len)
    f32 = jnp.float32
    in_vmem = pl.BlockSpec(memory_space=pltpu.VMEM)
    in_smem = pl.BlockSpec(memory_space=pltpu.SMEM)
    in_hbm = pl.BlockSpec(memory_space=pltpu.HBM)
    pieces = 2 * count

    packed, *blocks = pl.pallas_call(
        pack_kernel,
        out_shape=[jax.ShapeDtypeStruct((pieces, *block), f32)]
        + [jax.ShapeDtypeStruct(block, f32)] * pieces,
        in_specs=[in_smem, in_hbm, in_hbm],
        out_specs=[in_vmem] * (1 + pieces),
        scratch_shapes=[
            pltpu.VMEM(tiled, f32),
            pltpu.SemaphoreType.DMA((count,)),
            pltpu.SemaphoreType.DMA((2,)),
            pltpu.SemaphoreType.DMA((2,)),
        ],
        compiler_params=pltpu.CompilerParams(vmem_limit_bytes=8 << 20),
        cost_estimate=pl.CostEstimate(flops=1 << 20, bytes_accessed=4 << 20, transcendentals=0),
    )(mirror, *(pltpu.with_memory_space_constraint(x.reshape(tiled), pltpu.HBM) for x in (lesser, greater)))

    got = lax.all_to_all(packed, ("half", "en"), 0, 0, tiled=True)
    arrived = list(blocks)
    arrived[0] = pl.pallas_call(
        hold_kernel,
        out_shape=jax.ShapeDtypeStruct(block, f32),
        in_specs=[in_vmem],
        out_specs=in_vmem,
        compiler_params=pltpu.CompilerParams(vmem_limit_bytes=1 << 20),
    )(blocks[0])
    for s in far_first(count):
        route = [(d, d ^ s) for d in range(pieces)]
        arrived[s] = lax.ppermute(blocks[s], ("half", "en"), route)

    tables = (
        jnp.asarray(dft_block(1.0)),
        jnp.asarray(dft_block(length**-1.5)),
        jnp.asarray(twiddles(points)),
    )
    settings = dict(
        out_shape=jax.ShapeDtypeStruct((count, *block), f32),
        out_specs=in_vmem,
        compiler_params=pltpu.CompilerParams(vmem_limit_bytes=16 << 20),
        cost_estimate=pl.CostEstimate(
            flops=3 * 2 * 3 * points * SUBLANES * 4 * LANES * LANES,
            bytes_accessed=4 << 20,
            transcendentals=0,
        ),
    )
    scratch = [
        pltpu.VMEM((points, 2, SUBLANES, LANES), f32),
        pltpu.VMEM((2, points * SUBLANES, 2 * LANES), jnp.bfloat16),
        pltpu.VMEM((points * SUBLANES, 2 * LANES), f32),
        pltpu.VMEM((points * SUBLANES, 2 * LANES), f32),
    ]
    result_a = pl.pallas_call(
        correlate, in_specs=[in_vmem] * 4, scratch_shapes=scratch, **settings
    )(got, *tables)
    back_a = lax.all_to_all(result_a, "en", 0, 0, tiled=True)
    result_b = pl.pallas_call(
        functools.partial(correlate_pieces, pieces),
        in_specs=[in_vmem] * (pieces + 3),
        scratch_shapes=scratch + [pltpu.VMEM((pieces, *block), f32)],
        **settings,
    )(*arrived, *tables)
    back_b = lax.all_to_all(result_b, "en", 0, 0, tiled=True)

    def unpack(chunk, returned, *held):
        return pl.pallas_call(
            functools.partial(unpack_kernel, chunk),
            out_shape=jax.ShapeDtypeStruct(tiled, f32),
            in_specs=[in_vmem] + [in_hbm] * len(held),
            out_specs=in_hbm,
            scratch_shapes=[pltpu.SemaphoreType.DMA((2,))],
            input_output_aliases={1: 0} if held else {},
            compiler_params=pltpu.CompilerParams(vmem_limit_bytes=1 << 20),
        )(returned, *held)

    kept = unpack(0, back_a)
    out = unpack(1, back_b, kept)
    return out.reshape(2, group_rows, local_len)


def solution(mesh):
    groups = mesh.shape["grp"]
    devices = mesh.devices.reshape(2, groups // 2, mesh.shape["en"])
    finer = Mesh(devices, ("half", "grp", "en"))
    spec = P(None, ("half", "grp"), "en")
    in_specs = (spec, spec, P(("half", "grp")))

    return jax.shard_map(body, mesh=finer, in_specs=in_specs, out_specs=spec, check_vma=False)
```

time: 59.3 us -> 71.8 us (1.21)
  blocking collectives: 51.8 us -> 21.6 us
  starting transfers between devices: 0 us -> 28.1 us
  waiting for transfers between devices: 0 us -> 13.7 us
  Pallas kernels: 4.17 us -> 7.21 us
  local copies, waits for them, and re-layouts: 2.95 us -> 0.68 us
    ppermute x0 -> x15, starting transfers between devices: none -> 20.8 us  [body(): arrived[s] = lax.ppermute(blocks[s], ('half', 'en'), route)]
    all_to_all x1 -> x0, blocking collectives: 19.3 us -> none  [body(): returned = lax.all_to_all(result, 'en', 0, 0, tiled=True)]
    all_to_all x1, blocking collectives: 32.5 us -> 21.6 us  [body(): got = lax.all_to_all(packed, ('half', 'en'), 0, 0, tiled=True)]
    all_to_all x0 -> x2, waiting for transfers between devices: none -> 8.91 us  [the longest x1 8.91 us: body(): back_b = lax.all_to_all(result_b, 'en', 0, 0, tiled=True)]
    all_to_all x0 -> x2, starting transfers between devices: none -> 7.29 us  [the longest x1 3.88 us: body(): back_a = lax.all_to_all(result_a, 'en', 0, 0, tiled=True)]
    ppermute x0 -> x15, waiting for transfers between devices: none -> 4.8 us  [body(): arrived[s] = lax.ppermute(blocks[s], ('half', 'en'), route)]
    pallas_call x2 -> x6, Pallas kernels: 4.17 us -> 7.21 us  [the longest x1 2.21 us: body(): pl.pallas_call(pack_kernel, out_shape=[jax.ShapeDtypeStruct((pieces, *blo...]
    unnamed x12 -> x8, local copies, waits for them, and re-layouts: 2.11 us -> 0.68 us
  transfers between devices with their start and end apart: 0 -> 17, of which waited for: 0 -> 5; matrix products, arithmetic and copies ran while one was open for 0% -> 0% of each run, Pallas kernels for 0% -> 4%
where the time goes in v2:
time: 71.8 us; the launch traced here: 71.4 us
  starting transfers between devices  28.1 us (39%)
  blocking collectives  21.6 us (30%)
  waiting for transfers between devices  13.7 us (19%)
  Pallas kernels  7.21 us (10%)
    all_to_all x1, blocking collectives, body(): got = lax.all_to_all(packed, ('half', 'en'), 0, 0, tiled=True)  21.6 us
    ppermute x15, starting transfers between devices, body(): arrived[s] = lax.ppermute(blocks[s], ('half', 'en'), route)  20.8 us
    all_to_all x1, waiting for transfers between devices, body(): back_b = lax.all_to_all(result_b, 'en', 0, 0, tiled=True)  8.91 us
    ppermute x15, waiting for transfers between devices, body(): arrived[s] = lax.ppermute(blocks[s], ('half', 'en'), route)  4.8 us
    all_to_all x1, starting transfers between devices, body(): back_a = lax.all_to_all(result_a, 'en', 0, 0, tiled=True)  3.88 us
    all_to_all x1, starting transfers between devices, body(): back_b = lax.all_to_all(result_b, 'en', 0, 0, tiled=True)  3.41 us
    pallas_call x1, Pallas kernels, body(): pl.pallas_call(pack_kernel, out_shape=[jax.ShapeDtypeStruct((pieces, *blo...  2.21 us
    pallas_call x1, Pallas kernels, body(): pl.pallas_call(functools.partial(correlate_pieces, pieces), in_specs=[in_...  1.79 us
  transfers between devices with their start and end apart: 17, of which 5 were waited for; matrix products, arithmetic and copies ran while one was open for 0% of the time, Pallas kernels for 4%

profile of v2, /device:TPU:0, one launch (start us, length us, event | category | flops | bytes accessed | tf_op | source)
XLA Modules:
  0.0 71.4 jit_solution(8078584652592999285)
XLA Ops:
  0.0 0.0 copy-start.3
  0.0 0.7 copy-done.3
  0.7 2.2 %shard_map.64 = (f32[16,2,8,512]{3,2,1,0:T(8,128)S(1)}, f32[2,8,512]{2,1,0:T(8,128)S(1)}, f32[2,8,512]{2,1,0:T(8,128)S(1)}, f32[2,8,512]{2,1,0:T(8,128)S(1)}, f3...) custom-call(s32[128]{0:T(128)S(1)} %copy-done.3, ...), custom_call_target="tpu_custom_call" | custom-call | flops 1048576 | bytes 4194304 | tf_op jit(solution)/shard_map/pallas_call | solution.py:234
  2.9 0.0 copy-start
  2.9 0.0 copy-start.1
  2.9 0.0 copy-start.2
  2.9 21.6 %all_to_all.15.got = f32[16,2,8,512]{3,2,1,0:T(8,128)S(1)} all-to-all(f32[16,2,8,512]{3,2,1,0:T(8,128)S(1)} %get-tuple-element.38), channel_id=1, replica_groups=mesh['half'=2,'grp'=2,'en'=8] {'half','en'}, dimensions={0} | all-to-all | bytes 1048576 | tf_op jit(solution)/shard_map/all_to_all | solution.py:250
  24.5 0.0 copy-done
  24.5 0.0 copy-done.1
  24.5 0.0 copy-done.2
  24.5 1.8 %shard_map.67 = f32[8,2,8,512]{3,2,1,0:T(8,128)} custom-call(f32[16,2,8,512]{3,2,1,0:T(8,128)S(1)} %all_to_all.15.got, bf16[2,256,256]{2,1,0:T(8,128)(2,1)S(1)} %copy-done, bf16[2,256,256]{2,1,0:T(8,128)(2,1)S(1)} %copy-done.1, f32[2,32,128]{2,1,0:T(8,128)S(1)} %copy-done.2), custom_call_target="tpu_custom_call" | custom-call | flops 301989888 | bytes 4194304 | tf_op jit(solution)/shard_map/pallas_call | solution.py:284
  26.3 3.9 %all-to-all-start.2 = ((f32[8,2,8,512]{3,2,1,0:T(8,128)}), f32[8,2,8,512]{3,2,1,0:T(8,128)S(1)}, u32[]{:S(2)}, u32[]{:S(2)}) async-start(f32[8,2,8,512]{3,2,1,0:T(8,128)} %shard_map.67), calls=%async_computation.2 | async-start | bytes 524288 | tf_op jit(solution)/shard_map/all_to_all | solution.py:287
  30.1 0.5 collective-permute-start
  30.7 1.6 %collective-permute-start.1 = (f32[2,8,512]{2,1,0:T(8,128)S(1)}, f32[2,8,512]{2,1,0:T(8,128)S(1)}, u32[]{:S(2)}, u32[]{:S(2)}) collective-permute-start(f32[2,8,512]{2,1,0:T(8,128)S(1)} %get-tuple-element.24), channel_id=1, source_target_pairs={{0,2},{1,3},{2,0},{3,1},{4,6},{5,7},{6,4},{7,5},{16,18},{17,19},{1... | collective-permute-start | bytes 98312 | tf_op jit(solution)/shard_map/ppermute | solution.py:261
  32.3 0.2 collective-permute-start.10
  32.5 3.3 %collective-permute-start.11 = (f32[2,8,512]{2,1,0:T(8,128)S(1)}, f32[2,8,512]{2,1,0:T(8,128)S(1)}, u32[]{:S(2)}, u32[]{:S(2)}) collective-permute-start(f32[2,8,512]{2,1,0:T(8,128)S(1)} %get-tuple-element.34), channel_id=1, source_target_pairs={{0,20},{1,21},{2,22},{3,23},{4,16},{5,17},{6,18},{7,19},{16,4},{17... | collective-permute-start | bytes 98312 | tf_op jit(solution)/shard_map/ppermute | solution.py:261
  35.8 0.5 collective-permute-start.12
  36.4 0.0 collective-permute-done.refs_1_
  36.4 3.9 %collective-permute-start.13 = (f32[2,8,512]{2,1,0:T(8,128)S(1)}, f32[2,8,512]{2,1,0:T(8,128)S(1)}, u32[]{:S(2)}, u32[]{:S(2)}) collective-permute-start(f32[2,8,512]{2,1,0:T(8,128)S(1)} %get-tuple-element.36), channel_id=1, source_target_pairs={{0,22},{1,23},{2,20},{3,21},{4,18},{5,19},{6,16},{7,17},{16,6},{17... | collective-permute-start | bytes 98312 | tf_op jit(solution)/shard_map/ppermute | solution.py:261
  40.3 0.0 collective-permute-done.1.refs_2_
  40.3 0.2 collective-permute-start.14
  40.5 0.0 collective-permute-done.10.refs_11_
  40.5 1.1 %collective-permute-start.2 = (f32[2,8,512]{2,1,0:T(8,128)S(1)}, f32[2,8,512]{2,1,0:T(8,128)S(1)}, u32[]{:S(2)}, u32[]{:S(2)}) collective-permute-start(f32[2,8,512]{2,1,0:T(8,128)S(1)} %get-tuple-element.25), channel_id=1, source_target_pairs={{0,3},{1,2},{2,1},{3,0},{4,7},{5,6},{6,5},{7,4},{16,19},{17,18},{1... | collective-permute-start | bytes 98312 | tf_op jit(solution)/shard_map/ppermute | solution.py:261
  41.6 0.0 collective-permute-done.11.refs_12_
  41.6 2.9 %collective-permute-start.3 = (f32[2,8,512]{2,1,0:T(8,128)S(1)}, f32[2,8,512]{2,1,0:T(8,128)S(1)}, u32[]{:S(2)}, u32[]{:S(2)}) collective-permute-start(f32[2,8,512]{2,1,0:T(8,128)S(1)} %get-tuple-element.26), channel_id=1, source_target_pairs={{0,4},{1,5},{2,6},{3,7},{4,0},{5,1},{6,2},{7,3},{16,20},{17,21},{1... | collective-permute-start | bytes 98312 | tf_op jit(solution)/shard_map/ppermute | solution.py:261
  44.5 0.0 collective-permute-done.12.refs_13_
  44.5 0.0 collective-permute-start.4
  44.5 0.0 collective-permute-done.13.refs_14_
  44.5 2.1 %collective-permute-start.5 = (f32[2,8,512]{2,1,0:T(8,128)S(1)}, f32[2,8,512]{2,1,0:T(8,128)S(1)}, u32[]{:S(2)}, u32[]{:S(2)}) collective-permute-start(f32[2,8,512]{2,1,0:T(8,128)S(1)} %get-tuple-element.28), channel_id=1, source_target_pairs={{0,6},{1,7},{2,4},{3,5},{4,2},{5,3},{6,0},{7,1},{16,22},{17,23},{1... | collective-permute-start | bytes 98312 | tf_op jit(solution)/shard_map/ppermute | solution.py:261
  46.7 0.0 collective-permute-done.14.refs_15_
  46.7 1.2 %collective-permute-start.6 = (f32[2,8,512]{2,1,0:T(8,128)S(1)}, f32[2,8,512]{2,1,0:T(8,128)S(1)}, u32[]{:S(2)}, u32[]{:S(2)}) collective-permute-start(f32[2,8,512]{2,1,0:T(8,128)S(1)} %get-tuple-element.29), channel_id=1, source_target_pairs={{0,7},{1,6},{2,5},{3,4},{4,3},{5,2},{6,1},{7,0},{16,23},{17,22},{1... | collective-permute-start | bytes 98312 | tf_op jit(solution)/shard_map/ppermute | solution.py:261
  47.8 0.0 collective-permute-done.2.refs_3_
  47.9 3.1 %collective-permute-start.7 = (f32[2,8,512]{2,1,0:T(8,128)S(1)}, f32[2,8,512]{2,1,0:T(8,128)S(1)}, u32[]{:S(2)}, u32[]{:S(2)}) collective-permute-start(f32[2,8,512]{2,1,0:T(8,128)S(1)} %get-tuple-element.30), channel_id=1, source_target_pairs={{0,16},{1,17},{2,18},{3,19},{4,20},{5,21},{6,22},{7,23},{16,0},{17... | collective-permute-start | bytes 98312 | tf_op jit(solution)/shard_map/ppermute | solution.py:261
  50.9 0.0 collective-permute-done.3.refs_4_
  50.9 0.0 collective-permute-start.8
  50.9 0.0 collective-permute-done.4.refs_5_
  50.9 0.1 collective-permute-start.9
  51.0 0.0 collective-permute-done.5.refs_6_
  51.0 0.8 %collective-permute-done.6.refs_7_ = f32[2,8,512]{2,1,0:T(8,128)S(1)} collective-permute-done((f32[2,8,512]{2,1,0:T(8,128)S(1)}, f32[2,8,512]{2,1,0:T(8,128)S(1)}, u32[]{:S(2)}, u32[]{:S(2)}) %collective-permute-start.6) | collective-permute-done | bytes 32800 | tf_op jit(solution)/shard_map/ppermute | solution.py:261
  51.9 0.9 %collective-permute-done.7.refs_8_ = f32[2,8,512]{2,1,0:T(8,128)S(1)} collective-permute-done((f32[2,8,512]{2,1,0:T(8,128)S(1)}, f32[2,8,512]{2,1,0:T(8,128)S(1)}, u32[]{:S(2)}, u32[]{:S(2)}) %collective-permute-start.7) | collective-permute-done | bytes 32800 | tf_op jit(solution)/shard_map/ppermute | solution.py:261
  52.8 1.5 %collective-permute-done.8.refs_9_ = f32[2,8,512]{2,1,0:T(8,128)S(1)} collective-permute-done((f32[2,8,512]{2,1,0:T(8,128)S(1)}, f32[2,8,512]{2,1,0:T(8,128)S(1)}, u32[]{:S(2)}, u32[]{:S(2)}) %collective-permute-start.8) | collective-permute-done | bytes 32800 | tf_op jit(solution)/shard_map/ppermute | solution.py:261
  54.3 1.5 %collective-permute-done.9.refs_10_ = f32[2,8,512]{2,1,0:T(8,128)S(1)} collective-permute-done((f32[2,8,512]{2,1,0:T(8,128)S(1)}, f32[2,8,512]{2,1,0:T(8,128)S(1)}, u32[]{:S(2)}, u32[]{:S(2)}) %collective-permute-start.9) | collective-permute-done | bytes 32800 | tf_op jit(solution)/shard_map/ppermute | solution.py:261
  55.8 1.8 %shard_map.66 = f32[8,2,8,512]{3,2,1,0:T(8,128)} custom-call(f32[2,8,512]{2,1,0:T(8,128)S(1)} %shard_map.65.refs_0_, f32[2,8,512]{2,1,0:T(8,128)S(1)} %collective-permute-done.refs_1_, f32[2,8,512]{2,1,0:T(8,128)S(1)} %collective-permute-done.1.refs_2_, f32[2,8,512]{2,1,0:T(8,128)S(1)} %collective-permute-done.2.refs_3_, ...), custom_call_target="tpu_custom_call" | custom-call | flops 301989888 | bytes 4194304 | tf_op jit(solution)/shard_map/pallas_call | solution.py:288
  57.6 0.0 all-to-all-done.2.refs_0_
  57.6 3.4 %all-to-all-start = ((f32[8,2,8,512]{3,2,1,0:T(8,128)}), f32[8,2,8,512]{3,2,1,0:T(8,128)S(1)}, u32[]{:S(2)}, u32[]{:S(2)}) async-start(f32[8,2,8,512]{3,2,1,0:T(8,128)} %shard_map.66), calls=%async_computation | async-start | bytes 524288 | tf_op jit(solution)/shard_map/all_to_all | solution.py:294
  61.0 0.7 %shard_map.68.refs_1_ = f32[2,8,2,8,512]{4,3,2,1,0:T(8,128)} custom-call(f32[8,2,8,512]{3,2,1,0:T(8,128)S(1)} %all-to-all-done.2.refs_0_), custom_call_target="tpu_custom_call" | custom-call | tf_op jit(solution)/shard_map/pallas_call | solution.py:297
  61.7 8.9 %all-to-all-done.refs_0_ = f32[8,2,8,512]{3,2,1,0:T(8,128)S(1)} async-done(((f32[8,2,8,512]{3,2,1,0:T(8,128)}), f32[8,2,8,512]{3,2,1,0:T(8,128)S(1)}, u32[]{:S(2)}, u32[]{:S(2)}) %all-to-all-start) | async-done | bytes 262176 | tf_op jit(solution)/shard_map/all_to_all | solution.py:294
  70.6 0.7 %shard_map.69 = f32[2,8,2,8,512]{4,3,2,1,0:T(8,128)} custom-call(f32[8,2,8,512]{3,2,1,0:T(8,128)S(1)} %all-to-all-done.refs_0_, f32[2,8,2,8,512]{4,3,2,1,0:T(8,128)} %shard_map.68.refs_1_), custom_call_target="tpu_custom_call", output_to_operand_aliasing={{}: (1, {})} | custom-call | tf_op jit(solution)/shard_map/pallas_call | solution.py:297
  (1 shorter events, 0.0 us)
Async XLA Ops:
  0.0 0.7 copy-start.3
  2.9 21.6 %copy-start = (bf16[2,256,256]{2,1,0:T(8,128)(2,1)S(1)}, bf16[2,256,256]{2,1,0:T(8,128)(2,1)}, u32[]{:S(2)}) copy-start(bf16[2,256,256]{2,1,0:T(8,128)(2,1)} %constant.6.clone.refs_16_.forward) | copy-start | bytes 786436
  2.9 21.6 %copy-start.1 = (bf16[2,256,256]{2,1,0:T(8,128)(2,1)S(1)}, bf16[2,256,256]{2,1,0:T(8,128)(2,1)}, u32[]{:S(2)}) copy-start(bf16[2,256,256]{2,1,0:T(8,128)(2,1)} %constant.7.clone.refs_17_.backward) | copy-start | bytes 786436
  2.9 21.6 %copy-start.2 = (f32[2,32,128]{2,1,0:T(8,128)S(1)}, f32[2,32,128]{2,1,0:T(8,128)}, u32[]{:S(2)}) copy-start(f32[2,32,128]{2,1,0:T(8,128)} %constant.8.clone.refs_18_.twist) | copy-start | bytes 98308
  26.3 31.3 %all-to-all-start.2 = ((f32[8,2,8,512]{3,2,1,0:T(8,128)}), f32[8,2,8,512]{3,2,1,0:T(8,128)S(1)}, u32[]{:S(2)}, u32[]{:S(2)}) async-start(f32[8,2,8,512]{3,2,1,0:T(8,128)} %shard_map.67), calls=%async_computation.2 | async-start | bytes 524288 | tf_op jit(solution)/shard_map/all_to_all | solution.py:287
  30.1 6.2 %collective-permute-start = (f32[2,8,512]{2,1,0:T(8,128)S(1)}, f32[2,8,512]{2,1,0:T(8,128)S(1)}, u32[]{:S(2)}, u32[]{:S(2)}) collective-permute-start(f32[2,8,512]{2,1,0:T(8,128)S(1)} %get-tuple-element.23), channel_id=1, source_target_pairs={{0,1},{1,0},{2,3},{3,2},{4,5},{5,4},{6,7},{7,6},{16,17},{17,16},{1... | collective-permute-start | bytes 98312 | tf_op jit(solution)/shard_map/ppermute | solution.py:261
  30.7 9.6 %collective-permute-start.1 = (f32[2,8,512]{2,1,0:T(8,128)S(1)}, f32[2,8,512]{2,1,0:T(8,128)S(1)}, u32[]{:S(2)}, u32[]{:S(2)}) collective-permute-start(f32[2,8,512]{2,1,0:T(8,128)S(1)} %get-tuple-element.24), channel_id=1, source_target_pairs={{0,2},{1,3},{2,0},{3,1},{4,6},{5,7},{6,4},{7,5},{16,18},{17,19},{1... | collective-permute-start | bytes 98312 | tf_op jit(solution)/shard_map/ppermute | solution.py:261
  32.3 8.2 %collective-permute-start.10 = (f32[2,8,512]{2,1,0:T(8,128)S(1)}, f32[2,8,512]{2,1,0:T(8,128)S(1)}, u32[]{:S(2)}, u32[]{:S(2)}) collective-permute-start(f32[2,8,512]{2,1,0:T(8,128)S(1)} %get-tuple-element.33), channel_id=1, source_target_pairs={{0,19},{1,18},{2,17},{3,16},{4,23},{5,22},{6,21},{7,20},{16,3},{17... | collective-permute-start | bytes 98312 | tf_op jit(solution)/shard_map/ppermute | solution.py:261
  32.5 9.1 %collective-permute-start.11 = (f32[2,8,512]{2,1,0:T(8,128)S(1)}, f32[2,8,512]{2,1,0:T(8,128)S(1)}, u32[]{:S(2)}, u32[]{:S(2)}) collective-permute-start(f32[2,8,512]{2,1,0:T(8,128)S(1)} %get-tuple-element.34), channel_id=1, source_target_pairs={{0,20},{1,21},{2,22},{3,23},{4,16},{5,17},{6,18},{7,19},{16,4},{17... | collective-permute-start | bytes 98312 | tf_op jit(solution)/shard_map/ppermute | solution.py:261
  35.8 8.7 %collective-permute-start.12 = (f32[2,8,512]{2,1,0:T(8,128)S(1)}, f32[2,8,512]{2,1,0:T(8,128)S(1)}, u32[]{:S(2)}, u32[]{:S(2)}) collective-permute-start(f32[2,8,512]{2,1,0:T(8,128)S(1)} %get-tuple-element.35), channel_id=1, source_target_pairs={{0,21},{1,20},{2,23},{3,22},{4,17},{5,16},{6,19},{7,18},{16,5},{17... | collective-permute-start | bytes 98312 | tf_op jit(solution)/shard_map/ppermute | solution.py:261
  36.4 8.1 %collective-permute-start.13 = (f32[2,8,512]{2,1,0:T(8,128)S(1)}, f32[2,8,512]{2,1,0:T(8,128)S(1)}, u32[]{:S(2)}, u32[]{:S(2)}) collective-permute-start(f32[2,8,512]{2,1,0:T(8,128)S(1)} %get-tuple-element.36), channel_id=1, source_target_pairs={{0,22},{1,23},{2,20},{3,21},{4,18},{5,19},{6,16},{7,17},{16,6},{17... | collective-permute-start | bytes 98312 | tf_op jit(solution)/shard_map/ppermute | solution.py:261
  40.3 6.4 %collective-permute-start.14 = (f32[2,8,512]{2,1,0:T(8,128)S(1)}, f32[2,8,512]{2,1,0:T(8,128)S(1)}, u32[]{:S(2)}, u32[]{:S(2)}) collective-permute-start(f32[2,8,512]{2,1,0:T(8,128)S(1)} %get-tuple-element.37), channel_id=1, source_target_pairs={{0,23},{1,22},{2,21},{3,20},{4,19},{5,18},{6,17},{7,16},{16,7},{17... | collective-permute-start | bytes 98312 | tf_op jit(solution)/shard_map/ppermute | solution.py:261
  40.5 7.3 %collective-permute-start.2 = (f32[2,8,512]{2,1,0:T(8,128)S(1)}, f32[2,8,512]{2,1,0:T(8,128)S(1)}, u32[]{:S(2)}, u32[]{:S(2)}) collective-permute-start(f32[2,8,512]{2,1,0:T(8,128)S(1)} %get-tuple-element.25), channel_id=1, source_target_pairs={{0,3},{1,2},{2,1},{3,0},{4,7},{5,6},{6,5},{7,4},{16,19},{17,18},{1... | collective-permute-start | bytes 98312 | tf_op jit(solution)/shard_map/ppermute | solution.py:261
  41.6 9.3 %collective-permute-start.3 = (f32[2,8,512]{2,1,0:T(8,128)S(1)}, f32[2,8,512]{2,1,0:T(8,128)S(1)}, u32[]{:S(2)}, u32[]{:S(2)}) collective-permute-start(f32[2,8,512]{2,1,0:T(8,128)S(1)} %get-tuple-element.26), channel_id=1, source_target_pairs={{0,4},{1,5},{2,6},{3,7},{4,0},{5,1},{6,2},{7,3},{16,20},{17,21},{1... | collective-permute-start | bytes 98312 | tf_op jit(solution)/shard_map/ppermute | solution.py:261
  44.5 6.4 %collective-permute-start.4 = (f32[2,8,512]{2,1,0:T(8,128)S(1)}, f32[2,8,512]{2,1,0:T(8,128)S(1)}, u32[]{:S(2)}, u32[]{:S(2)}) collective-permute-start(f32[2,8,512]{2,1,0:T(8,128)S(1)} %get-tuple-element.27), channel_id=1, source_target_pairs={{0,5},{1,4},{2,7},{3,6},{4,1},{5,0},{6,3},{7,2},{16,21},{17,20},{1... | collective-permute-start | bytes 98312 | tf_op jit(solution)/shard_map/ppermute | solution.py:261
  44.5 6.5 %collective-permute-start.5 = (f32[2,8,512]{2,1,0:T(8,128)S(1)}, f32[2,8,512]{2,1,0:T(8,128)S(1)}, u32[]{:S(2)}, u32[]{:S(2)}) collective-permute-start(f32[2,8,512]{2,1,0:T(8,128)S(1)} %get-tuple-element.28), channel_id=1, source_target_pairs={{0,6},{1,7},{2,4},{3,5},{4,2},{5,3},{6,0},{7,1},{16,22},{17,23},{1... | collective-permute-start | bytes 98312 | tf_op jit(solution)/shard_map/ppermute | solution.py:261
  46.7 5.2 %collective-permute-start.6 = (f32[2,8,512]{2,1,0:T(8,128)S(1)}, f32[2,8,512]{2,1,0:T(8,128)S(1)}, u32[]{:S(2)}, u32[]{:S(2)}) collective-permute-start(f32[2,8,512]{2,1,0:T(8,128)S(1)} %get-tuple-element.29), channel_id=1, source_target_pairs={{0,7},{1,6},{2,5},{3,4},{4,3},{5,2},{6,1},{7,0},{16,23},{17,22},{1... | collective-permute-start | bytes 98312 | tf_op jit(solution)/shard_map/ppermute | solution.py:261
  47.9 4.9 %collective-permute-start.7 = (f32[2,8,512]{2,1,0:T(8,128)S(1)}, f32[2,8,512]{2,1,0:T(8,128)S(1)}, u32[]{:S(2)}, u32[]{:S(2)}) collective-permute-start(f32[2,8,512]{2,1,0:T(8,128)S(1)} %get-tuple-element.30), channel_id=1, source_target_pairs={{0,16},{1,17},{2,18},{3,19},{4,20},{5,21},{6,22},{7,23},{16,0},{17... | collective-permute-start | bytes 98312 | tf_op jit(solution)/shard_map/ppermute | solution.py:261
  50.9 3.3 %collective-permute-start.8 = (f32[2,8,512]{2,1,0:T(8,128)S(1)}, f32[2,8,512]{2,1,0:T(8,128)S(1)}, u32[]{:S(2)}, u32[]{:S(2)}) collective-permute-start(f32[2,8,512]{2,1,0:T(8,128)S(1)} %get-tuple-element.31), channel_id=1, source_target_pairs={{0,17},{1,16},{2,19},{3,18},{4,21},{5,20},{6,23},{7,22},{16,1},{17... | collective-permute-start | bytes 98312 | tf_op jit(solution)/shard_map/ppermute | solution.py:261
  50.9 4.9 %collective-permute-start.9 = (f32[2,8,512]{2,1,0:T(8,128)S(1)}, f32[2,8,512]{2,1,0:T(8,128)S(1)}, u32[]{:S(2)}, u32[]{:S(2)}) collective-permute-start(f32[2,8,512]{2,1,0:T(8,128)S(1)} %get-tuple-element.32), channel_id=1, source_target_pairs={{0,18},{1,19},{2,16},{3,17},{4,22},{5,23},{6,20},{7,21},{16,2},{17... | collective-permute-start | bytes 98312 | tf_op jit(solution)/shard_map/ppermute | solution.py:261
  57.6 13.1 %all-to-all-start = ((f32[8,2,8,512]{3,2,1,0:T(8,128)}), f32[8,2,8,512]{3,2,1,0:T(8,128)S(1)}, u32[]{:S(2)}, u32[]{:S(2)}) async-start(f32[8,2,8,512]{3,2,1,0:T(8,128)} %shard_map.66), calls=%async_computation | async-start | bytes 524288 | tf_op jit(solution)/shard_map/all_to_all | solution.py:294

commit v3 on v2

--- a/solution.py
+++ b/solution.py
@@ -102,49 +102,80 @@
     return re * cos - im * sin, re * sin + im * cos
 
 
-def pack_kernel(mirror, lesser, greater, packed, *rest):
-    blocks, (held, block_sems, chunk_sems, held_sems) = rest[:-4], rest[-4:]
+def pack_kernel(mirror, lesser, greater, packed, second, places, held, ready, sems):
     _, count, tiles, sub, local_len = lesser.shape
     rows = tiles * sub
     own = lax.axis_index("half")
+    loads = [pltpu.make_async_copy(mirror, places, sems.at[0])]
+    loads += [pltpu.make_async_copy(greater.at[p], held.at[p], sems.at[1 + p]) for p in range(2)]
+    firsts = [
+        pltpu.make_async_copy(lesser.at[p, :, 0], ready.at[0, :, p], sems.at[3 + p])
+        for p in range(2)
+    ]
+    for copy in loads + firsts:
+        copy.start()
+    stores = [
+        pltpu.make_async_copy(ready.at[0], packed.at[pl.ds(own * count, count)], sems.at[5]),
+        pltpu.make_async_copy(ready.at[1], packed.at[pl.ds((1 - own) * count, count)], sems.at[6]),
+    ]
+    loads[0].wait()
+    lane = lax.broadcasted_iota(jnp.int32, (rows, count * rows), 1)
+    line = lax.broadcasted_iota(jnp.int32, (rows, count * rows), 0)
+    goal = jnp.broadcast_to(places[...], (rows, count * rows)) % rows
+    source = jnp.where(goal == line, (lane % rows).astype(jnp.float32), 0.0)
+    orders = [
+        jnp.sum(jnp.where(lane // rows == to, source, 0.0), axis=1, keepdims=True).astype(jnp.int32)
+        for to in range(count)
+    ]
+    for copy in firsts:
+        copy.wait()
+    stores[0].start()
+    for part in range(2):
+        loads[1 + part].wait()
+        for to in range(count):
+            order = jnp.broadcast_to(orders[to], (rows, LANES))
+            for start in range(0, local_len, LANES):
+                span = slice(start, start + LANES)
+                tiles_in = [held[part, to, u, :, span] for u in range(tiles)]
+                for t in range(tiles):
+                    wanted = order[t * sub : (t + 1) * sub]
+                    moved = jnp.zeros((sub, LANES), jnp.float32)
+                    for u, tile in enumerate(tiles_in):
+                        picked = jnp.take_along_axis(tile, wanted % sub, axis=0)
+                        moved = jnp.where(wanted // sub == u, picked, moved)
+                    if t == 0:
+                        ready[1, to, part, :, span] = moved
+                    else:
+                        second[to, part, :, span] = moved
+    stores[1].start()
+    for copy in stores:
+        copy.wait()
+
+
+def split_kernel(lesser, second, mine, give, sems):
+    chips = mine.shape[1]
     me = lax.axis_index("en")
-    loads = [pltpu.make_async_copy(greater.at[p], held.at[p], held_sems.at[p]) for p in range(2)]
-    moves = [
-        pltpu.make_async_copy(
-            lesser.at[p, :, 0], packed.at[pl.ds(own * count, count), p], chunk_sems.at[p]
-        )
-        for p in range(2)
-    ]
-    moves += [
-        pltpu.make_async_copy(lesser.at[:, me ^ s, 1], blocks[s], block_sems.at[s])
-        for s in range(count)
-    ]
-    for copy in loads + moves:
+    copies = []
+    for z in range(chips):
+        for core, target in enumerate((mine, give)):
+            to = me ^ (2 * z + core)
+            copies.append(
+                pltpu.make_async_copy(lesser.at[:, to, 1], target.at[0, z], sems.at[core, z])
+            )
+    for copy in copies:
         copy.start()
-    line = lax.broadcasted_iota(jnp.int32, (sub, LANES), 0)
-    for copy in loads:
+    for z in range(chips):
+        for core, target in enumerate((mine, give)):
+            target[1, z] = second[me ^ (2 * z + core)]
+    for copy in copies:
         copy.wait()
-    for s in range(count):
-        to = me ^ s
-        orders = [jnp.zeros((sub, LANES), jnp.int32) for _ in range(tiles)]
-        for row in range(rows):
-            place = mirror[to * rows + row] % rows
-            orders = [jnp.where(line + t * sub == place, row, o) for t, o in enumerate(orders)]
-        for part in range(2):
-            for lane in range(0, local_len, LANES):
-                span = slice(lane, lane + LANES)
-                sources = [held[part, to, t, :, span] for t in range(tiles)]
-                for t, order in enumerate(orders):
-                    moved = jnp.zeros((sub, LANES), jnp.float32)
-                    for u, source in enumerate(sources):
-                        picked = jnp.take_along_axis(source, order % sub, axis=0)
-                        moved = jnp.where(order // sub == u, picked, moved)
-                    if t == 0:
-                        packed[(1 - own) * count + to, part, :, span] = moved
-                    else:
-                        blocks[count + s][part, :, span] = moved
-    for copy in moves:
-        copy.wait()
+
+
+def join_kernel(mine, got, *outs):
+    chips = mine.shape[1]
+    for t, out in enumerate(outs):
+        out[0] = mine[t // chips, t % chips]
+        out[1] = got[t // chips, t % chips]
 
 
 def correlate(got, forward, backward, twist, out, keep, halves, left, right):
@@ -188,12 +219,13 @@
 
 def correlate_pieces(pieces, *refs):
     got, blocks, rest = refs[-1], refs[:pieces], refs[pieces:-1]
-    count = pieces // 2
+    chips = pieces // 2
     own = lax.axis_index("half")
     me = lax.axis_index("en")
-    for s, block in enumerate(blocks):
-        half = own if s < count else 1 - own
-        got[half * count + (me ^ (s % count))] = block[...]
+    for t, block in enumerate(blocks):
+        half = own if t < chips else 1 - own
+        for core in range(2):
+            got[half * (2 * chips) + (me ^ (2 * (t % chips) + core))] = block[core]
     correlate(got, *rest)
 
 
@@ -201,8 +233,8 @@
     out[...] = block[...]
 
 
-def far_first(count):
-    return sorted(range(1, 2 * count), key=lambda s: (-(s % count // 2), s < count, s))
+def far_first(chips):
+    return sorted(range(1, 2 * chips), key=lambda t: (-(t % chips), t < chips))
 
 
 def unpack_kernel(chunk, *refs):
@@ -229,36 +261,59 @@
     in_vmem = pl.BlockSpec(memory_space=pltpu.VMEM)
     in_smem = pl.BlockSpec(memory_space=pltpu.SMEM)
     in_hbm = pl.BlockSpec(memory_space=pltpu.HBM)
-    pieces = 2 * count
-
-    packed, *blocks = pl.pallas_call(
+
+    chips = count // 2
+    half_view = (2, chips, *block)
+    bundle = jax.ShapeDtypeStruct((2, *block), f32)
+    mirror, lesser, greater = (
+        pltpu.with_memory_space_constraint(x, pltpu.HBM)
+        for x in (mirror[None], lesser.reshape(tiled), greater.reshape(tiled))
+    )
+    packed, second = pl.pallas_call(
         pack_kernel,
-        out_shape=[jax.ShapeDtypeStruct((pieces, *block), f32)]
-        + [jax.ShapeDtypeStruct(block, f32)] * pieces,
-        in_specs=[in_smem, in_hbm, in_hbm],
-        out_specs=[in_vmem] * (1 + pieces),
+        out_shape=[
+            jax.ShapeDtypeStruct((2 * count, *block), f32),
+            jax.ShapeDtypeStruct((count, *block), f32),
+        ],
+        in_specs=[in_hbm] * 3,
+        out_specs=[in_hbm, in_vmem],
         scratch_shapes=[
+            pltpu.VMEM((1, group_rows), jnp.int32),
             pltpu.VMEM(tiled, f32),
-            pltpu.SemaphoreType.DMA((count,)),
-            pltpu.SemaphoreType.DMA((2,)),
-            pltpu.SemaphoreType.DMA((2,)),
+            pltpu.VMEM((2, count, *block), f32),
+            pltpu.SemaphoreType.DMA((7,)),
         ],
         compiler_params=pltpu.CompilerParams(vmem_limit_bytes=8 << 20),
-        cost_estimate=pl.CostEstimate(flops=1 << 20, bytes_accessed=4 << 20, transcendentals=0),
-    )(mirror, *(pltpu.with_memory_space_constraint(x.reshape(tiled), pltpu.HBM) for x in (lesser, greater)))
-
+    )(mirror, lesser, greater)
     got = lax.all_to_all(packed, ("half", "en"), 0, 0, tiled=True)
-    arrived = list(blocks)
+    mine, give = pl.pallas_call(
+        split_kernel,
+        out_shape=[jax.ShapeDtypeStruct(half_view, f32)] * 2,
+        in_specs=[in_hbm, in_vmem],
+        out_specs=[in_vmem] * 2,
+        scratch_shapes=[pltpu.SemaphoreType.DMA((2, chips))],
+        compiler_params=pltpu.CompilerParams(vmem_limit_bytes=4 << 20),
+    )(lesser, second)
+    given = lax.ppermute(give, "en", [(e, e ^ 1) for e in range(count)])
+    bundles = pl.pallas_call(
+        join_kernel,
+        out_shape=[bundle] * (2 * chips),
+        in_specs=[in_vmem] * 2,
+        out_specs=[in_vmem] * (2 * chips),
+        compiler_params=pltpu.CompilerParams(vmem_limit_bytes=4 << 20),
+    )(mine, given)
+    arrived = list(bundles)
     arrived[0] = pl.pallas_call(
         hold_kernel,
-        out_shape=jax.ShapeDtypeStruct(block, f32),
+        out_shape=bundle,
         in_specs=[in_vmem],
         out_specs=in_vmem,
         compiler_params=pltpu.CompilerParams(vmem_limit_bytes=1 << 20),
-    )(blocks[0])
-    for s in far_first(count):
-        route = [(d, d ^ s) for d in range(pieces)]
-        arrived[s] = lax.ppermute(blocks[s], ("half", "en"), route)
+    )(bundles[0])
+    for t in far_first(chips):
+        step = t // chips * count + 2 * (t % chips)
+        route = [(d, d ^ step) for d in range(2 * count)]
+        arrived[t] = lax.ppermute(bundles[t], ("half", "en"), route)
 
     tables = (
         jnp.asarray(dft_block(1.0)),
@@ -286,9 +341,9 @@
     )(got, *tables)
     back_a = lax.all_to_all(result_a, "en", 0, 0, tiled=True)
     result_b = pl.pallas_call(
-        functools.partial(correlate_pieces, pieces),
-        in_specs=[in_vmem] * (pieces + 3),
-        scratch_shapes=scratch + [pltpu.VMEM((pieces, *block), f32)],
+        functools.partial(correlate_pieces, 2 * chips),
+        in_specs=[in_vmem] * (2 * chips + 3),
+        scratch_shapes=scratch + [pltpu.VMEM((2 * count, *block), f32)],
         **settings,
     )(*arrived, *tables)
     back_b = lax.all_to_all(result_b, "en", 0, 0, tiled=True)

time: 71.8 us -> 66.2 us (0.922)
  starting transfers between devices: 28.1 us -> 19.2 us
  waiting for transfers between devices: 13.7 us -> 17.5 us
    ppermute x15 -> x8, starting transfers between devices: 20.8 us -> 11.9 us  [the longest x7 11.4 us: body(): arrived[t] = lax.ppermute(bundles[t], ('half', 'en'), route)]
    ppermute x15 -> x8, waiting for transfers between devices: 4.8 us -> 8.6 us  [the longest x7 7.43 us: body(): arrived[t] = lax.ppermute(bundles[t], ('half', 'en'), route)]
    pallas_call x3 -> x5, Pallas kernels: 4.01 us -> 4.12 us  [the longest x1 1.78 us: body(): pl.pallas_call(functools.partial(correlate_pieces, 2 * chips), in_specs=[...]
  transfers between devices with their start and end apart: 17 -> 10, of which waited for: 5 -> 5; matrix products, arithmetic and copies ran while one was open for 0% -> 0% of each run, Pallas kernels for 4% -> 5%
where the time goes in v3:
time: 66.2 us; the launch traced here: 65.7 us
  blocking collectives  21.6 us (33%)
  starting transfers between devices  19.2 us (29%)
  waiting for transfers between devices  17.5 us (26%)
  Pallas kernels  7.32 us (11%)
    all_to_all x1, blocking collectives, body(): got = lax.all_to_all(packed, ('half', 'en'), 0, 0, tiled=True)  21.6 us
    ppermute x7, starting transfers between devices, body(): arrived[t] = lax.ppermute(bundles[t], ('half', 'en'), route)  11.4 us
    all_to_all x1, waiting for transfers between devices, body(): back_b = lax.all_to_all(result_b, 'en', 0, 0, tiled=True)  8.91 us
    ppermute x7, waiting for transfers between devices, body(): arrived[t] = lax.ppermute(bundles[t], ('half', 'en'), route)  7.43 us
    all_to_all x1, starting transfers between devices, body(): back_a = lax.all_to_all(result_a, 'en', 0, 0, tiled=True)  3.88 us
    all_to_all x1, starting transfers between devices, body(): back_b = lax.all_to_all(result_b, 'en', 0, 0, tiled=True)  3.41 us
    pallas_call x1, Pallas kernels, body(): pl.pallas_call(functools.partial(correlate_pieces, 2 * chips), in_specs=[...  1.78 us
    pallas_call x1, Pallas kernels, body(): pl.pallas_call(correlate, in_specs=[in_vmem] * 4, scratch_shapes=scratch,...  1.77 us
  transfers between devices with their start and end apart: 10, of which 5 were waited for; matrix products, arithmetic and copies ran while one was open for 0% of the time, Pallas kernels for 5%

profile of v3, /device:TPU:0, one launch (start us, length us, event | category | flops | bytes accessed | tf_op | source)
XLA Modules:
  0.0 65.7 jit_solution(11974627535692576976)
XLA Ops:
  0.0 1.4 %shard_map.64 = (f32[16,2,8,512]{3,2,1,0:T(8,128)S(1)}, f32[8,2,8,512]{3,2,1,0:T(8,128)S(1)}) custom-call(s32[1,128]{1,0:T(1,128)} %bitcast.7, f32[2,8,2,8,512]{4,3,2,1,0:T(8,128)} %bitcast.4, f32[2,8,2,8,512]{4,3,2,1,0:T(8,128)} %bitcast.6), custom_call_target="tpu_custom_call" | custom-call | tf_op jit(solution)/shard_map/pallas_call | solution.py:272
  1.4 0.0 copy-start
  1.4 0.0 copy-start.1
  1.4 0.0 copy-start.2
  1.4 21.6 %all_to_all.15.got = f32[16,2,8,512]{3,2,1,0:T(8,128)S(1)} all-to-all(f32[16,2,8,512]{3,2,1,0:T(8,128)S(1)} %get-tuple-element.28), channel_id=1, replica_groups=mesh['half'=2,'grp'=2,'en'=8] {'half','en'}, dimensions={0} | all-to-all | bytes 1048576 | tf_op jit(solution)/shard_map/all_to_all | solution.py:288
  23.0 0.0 copy-done
  23.0 0.0 copy-done.1
  23.0 0.0 copy-done.2
  23.0 1.8 %shard_map.69 = f32[8,2,8,512]{3,2,1,0:T(8,128)} custom-call(f32[16,2,8,512]{3,2,1,0:T(8,128)S(1)} %all_to_all.15.got, bf16[2,256,256]{2,1,0:T(8,128)(2,1)S(1)} %copy-done.1, bf16[2,256,256]{2,1,0:T(8,128)(2,1)S(1)} %copy-done, f32[2,32,128]{2,1,0:T(8,128)S(1)} %copy-done.2), custom_call_target="tpu_custom_call" | custom-call | flops 301989888 | bytes 4194304 | tf_op jit(solution)/shard_map/pallas_call | solution.py:339
  24.8 3.9 %all-to-all-start.2 = ((f32[8,2,8,512]{3,2,1,0:T(8,128)}), f32[8,2,8,512]{3,2,1,0:T(8,128)S(1)}, u32[]{:S(2)}, u32[]{:S(2)}) async-start(f32[8,2,8,512]{3,2,1,0:T(8,128)} %shard_map.69), calls=%async_computation.2 | async-start | bytes 524288 | tf_op jit(solution)/shard_map/all_to_all | solution.py:342
  28.6 0.9 %shard_map.65 = (f32[2,4,2,8,512]{4,3,2,1,0:T(8,128)S(1)}, f32[2,4,2,8,512]{4,3,2,1,0:T(8,128)S(1)}) custom-call(f32[2,8,2,8,512]{4,3,2,1,0:T(8,128)} %bitcast.5, f32[8,2,8,512]{3,2,1,0:T(8,128)S(1)} %get-tuple-element.17.second), custom_call_target="tpu_custom_call" | custom-call | tf_op jit(solution)/shard_map/pallas_call | solution.py:289
  29.6 0.6 collective-permute-start
  30.2 1.2 %collective-permute-done.got = f32[2,4,2,8,512]{4,3,2,1,0:T(8,128)S(1)} collective-permute-done((f32[2,4,2,8,512]{4,3,2,1,0:T(8,128)S(1)}, f32[2,4,2,8,512]{4,3,2,1,0:T(8,128)S(1)}, u32[]{:S(2)}, u32[]{:S(2)}) %collective-permute-start) | collective-permute-done | bytes 262176 | tf_op jit(solution)/shard_map/ppermute | solution.py:297
  31.4 2.0 %collective-permute-start.1 = (f32[2,2,8,512]{3,2,1,0:T(8,128)S(1)}, f32[2,2,8,512]{3,2,1,0:T(8,128)S(1)}, u32[]{:S(2)}, u32[]{:S(2)}) collective-permute-start(f32[2,2,8,512]{3,2,1,0:T(8,128)S(1)} %get-tuple-element.21), channel_id=1, source_target_pairs={{0,2},{1,3},{2,0},{3,1},{4,6},{5,7},{6,4},{7,5},{16,18},{17,19},{1... | collective-permute-start | bytes 196616 | tf_op jit(solution)/shard_map/ppermute | solution.py:316
  33.3 2.4 %collective-permute-start.2 = (f32[2,2,8,512]{3,2,1,0:T(8,128)S(1)}, f32[2,2,8,512]{3,2,1,0:T(8,128)S(1)}, u32[]{:S(2)}, u32[]{:S(2)}) collective-permute-start(f32[2,2,8,512]{3,2,1,0:T(8,128)S(1)} %get-tuple-element.22), channel_id=1, source_target_pairs={{0,4},{1,5},{2,6},{3,7},{4,0},{5,1},{6,2},{7,3},{16,20},{17,21},{1... | collective-permute-start | bytes 196616 | tf_op jit(solution)/shard_map/ppermute | solution.py:316
  35.7 0.1 collective-permute-start.3
  35.8 0.9 %collective-permute-start.4 = (f32[2,2,8,512]{3,2,1,0:T(8,128)S(1)}, f32[2,2,8,512]{3,2,1,0:T(8,128)S(1)}, u32[]{:S(2)}, u32[]{:S(2)}) collective-permute-start(f32[2,2,8,512]{3,2,1,0:T(8,128)S(1)} %get-tuple-element.24), channel_id=1, source_target_pairs={{0,16},{1,17},{2,18},{3,19},{4,20},{5,21},{6,22},{7,23},{16,0},{17... | collective-permute-start | bytes 196616 | tf_op jit(solution)/shard_map/ppermute | solution.py:316
  36.7 1.5 %collective-permute-start.5 = (f32[2,2,8,512]{3,2,1,0:T(8,128)S(1)}, f32[2,2,8,512]{3,2,1,0:T(8,128)S(1)}, u32[]{:S(2)}, u32[]{:S(2)}) collective-permute-start(f32[2,2,8,512]{3,2,1,0:T(8,128)S(1)} %get-tuple-element.25), channel_id=1, source_target_pairs={{0,18},{1,19},{2,16},{3,17},{4,22},{5,23},{6,20},{7,21},{16,2},{17... | collective-permute-start | bytes 196616 | tf_op jit(solution)/shard_map/ppermute | solution.py:316
  38.3 0.0 collective-permute-done.1.refs_1_
  38.3 3.4 %collective-permute-start.6 = (f32[2,2,8,512]{3,2,1,0:T(8,128)S(1)}, f32[2,2,8,512]{3,2,1,0:T(8,128)S(1)}, u32[]{:S(2)}, u32[]{:S(2)}) collective-permute-start(f32[2,2,8,512]{3,2,1,0:T(8,128)S(1)} %get-tuple-element.26), channel_id=1, source_target_pairs={{0,20},{1,21},{2,22},{3,23},{4,16},{5,17},{6,18},{7,19},{16,4},{17... | collective-permute-start | bytes 196616 | tf_op jit(solution)/shard_map/ppermute | solution.py:316
  41.6 1.6 %collective-permute-done.2.refs_2_ = f32[2,2,8,512]{3,2,1,0:T(8,128)S(1)} collective-permute-done((f32[2,2,8,512]{3,2,1,0:T(8,128)S(1)}, f32[2,2,8,512]{3,2,1,0:T(8,128)S(1)}, u32[]{:S(2)}, u32[]{:S(2)}) %collective-permute-start.2) | collective-permute-done | bytes 65568 | tf_op jit(solution)/shard_map/ppermute | solution.py:316
  43.2 1.1 %collective-permute-start.7 = (f32[2,2,8,512]{3,2,1,0:T(8,128)S(1)}, f32[2,2,8,512]{3,2,1,0:T(8,128)S(1)}, u32[]{:S(2)}, u32[]{:S(2)}) collective-permute-start(f32[2,2,8,512]{3,2,1,0:T(8,128)S(1)} %get-tuple-element.27), channel_id=1, source_target_pairs={{0,22},{1,23},{2,20},{3,21},{4,18},{5,19},{6,16},{7,17},{16,6},{17... | collective-permute-start | bytes 196616 | tf_op jit(solution)/shard_map/ppermute | solution.py:316
  44.3 0.0 collective-permute-done.3.refs_3_
  44.3 0.0 collective-permute-done.4.refs_4_
  44.3 0.0 collective-permute-done.5.refs_5_
  44.4 3.7 %collective-permute-done.6.refs_6_ = f32[2,2,8,512]{3,2,1,0:T(8,128)S(1)} collective-permute-done((f32[2,2,8,512]{3,2,1,0:T(8,128)S(1)}, f32[2,2,8,512]{3,2,1,0:T(8,128)S(1)}, u32[]{:S(2)}, u32[]{:S(2)}) %collective-permute-start.6) | collective-permute-done | bytes 65568 | tf_op jit(solution)/shard_map/ppermute | solution.py:316
  48.0 2.1 %collective-permute-done.7.refs_7_ = f32[2,2,8,512]{3,2,1,0:T(8,128)S(1)} collective-permute-done((f32[2,2,8,512]{3,2,1,0:T(8,128)S(1)}, f32[2,2,8,512]{3,2,1,0:T(8,128)S(1)}, u32[]{:S(2)}, u32[]{:S(2)}) %collective-permute-start.7) | collective-permute-done | bytes 65568 | tf_op jit(solution)/shard_map/ppermute | solution.py:316
  50.2 1.8 %shard_map.68 = f32[8,2,8,512]{3,2,1,0:T(8,128)} custom-call(f32[2,2,8,512]{3,2,1,0:T(8,128)S(1)} %shard_map.67.refs_0_, f32[2,2,8,512]{3,2,1,0:T(8,128)S(1)} %collective-permute-done.1.refs_1_, f32[2,2,8,512]{3,2,1,0:T(8,128)S(1)} %collective-permute-done.2.refs_2_, f32[2,2,8,512]{3,2,1,0:T(8,128)S(1)} %collective-permute-done.3.refs_3_, ...), custom_call_target="tpu_custom_call" | custom-call | flops 301989888 | bytes 4194304 | tf_op jit(solution)/shard_map/pallas_call | solution.py:343
  52.0 0.0 all-to-all-done.2.refs_0_
  52.0 3.4 %all-to-all-start = ((f32[8,2,8,512]{3,2,1,0:T(8,128)}), f32[8,2,8,512]{3,2,1,0:T(8,128)S(1)}, u32[]{:S(2)}, u32[]{:S(2)}) async-start(f32[8,2,8,512]{3,2,1,0:T(8,128)} %shard_map.68), calls=%async_computation | async-start | bytes 524288 | tf_op jit(solution)/shard_map/all_to_all | solution.py:349
  55.4 0.7 %shard_map.70.refs_1_ = f32[2,8,2,8,512]{4,3,2,1,0:T(8,128)} custom-call(f32[8,2,8,512]{3,2,1,0:T(8,128)S(1)} %all-to-all-done.2.refs_0_), custom_call_target="tpu_custom_call" | custom-call | tf_op jit(solution)/shard_map/pallas_call | solution.py:352
  56.1 8.9 %all-to-all-done.refs_0_ = f32[8,2,8,512]{3,2,1,0:T(8,128)S(1)} async-done(((f32[8,2,8,512]{3,2,1,0:T(8,128)}), f32[8,2,8,512]{3,2,1,0:T(8,128)S(1)}, u32[]{:S(2)}, u32[]{:S(2)}) %all-to-all-start) | async-done | bytes 262176 | tf_op jit(solution)/shard_map/all_to_all | solution.py:349
  65.0 0.7 %shard_map.71 = f32[2,8,2,8,512]{4,3,2,1,0:T(8,128)} custom-call(f32[8,2,8,512]{3,2,1,0:T(8,128)S(1)} %all-to-all-done.refs_0_, f32[2,8,2,8,512]{4,3,2,1,0:T(8,128)} %shard_map.70.refs_1_), custom_call_target="tpu_custom_call", output_to_operand_aliasing={{}: (1, {})} | custom-call | tf_op jit(solution)/shard_map/pallas_call | solution.py:352
  (2 shorter events, 0.0 us)
Async XLA Ops:
  1.4 21.6 %copy-start = (bf16[2,256,256]{2,1,0:T(8,128)(2,1)S(1)}, bf16[2,256,256]{2,1,0:T(8,128)(2,1)}, u32[]{:S(2)}) copy-start(bf16[2,256,256]{2,1,0:T(8,128)(2,1)} %constant.7.clone.refs_9_.backward) | copy-start | bytes 786436
  1.4 21.6 %copy-start.1 = (bf16[2,256,256]{2,1,0:T(8,128)(2,1)S(1)}, bf16[2,256,256]{2,1,0:T(8,128)(2,1)}, u32[]{:S(2)}) copy-start(bf16[2,256,256]{2,1,0:T(8,128)(2,1)} %constant.6.clone.refs_8_.forward) | copy-start | bytes 786436
  1.4 21.6 %copy-start.2 = (f32[2,32,128]{2,1,0:T(8,128)S(1)}, f32[2,32,128]{2,1,0:T(8,128)}, u32[]{:S(2)}) copy-start(f32[2,32,128]{2,1,0:T(8,128)} %constant.8.clone.refs_10_.twist) | copy-start | bytes 98308
  24.8 27.2 %all-to-all-start.2 = ((f32[8,2,8,512]{3,2,1,0:T(8,128)}), f32[8,2,8,512]{3,2,1,0:T(8,128)S(1)}, u32[]{:S(2)}, u32[]{:S(2)}) async-start(f32[8,2,8,512]{3,2,1,0:T(8,128)} %shard_map.69), calls=%async_computation.2 | async-start | bytes 524288 | tf_op jit(solution)/shard_map/all_to_all | solution.py:342
  29.6 1.7 %collective-permute-start = (f32[2,4,2,8,512]{4,3,2,1,0:T(8,128)S(1)}, f32[2,4,2,8,512]{4,3,2,1,0:T(8,128)S(1)}, u32[]{:S(2)}, u32[]{:S(2)}) collective-permute-start(f32[2,4,2,8,512]{4,3,2,1,0:T(8,128)S(1)} %get-tuple-element.19), channel_id=1, source_target_pairs={{0,1},{1,0},{2,3},{3,2},{4,5},{5,4},{6,7},{7,6},{8,9},{9,8},{10,11... | collective-permute-start | bytes 786440 | tf_op jit(solution)/shard_map/ppermute | solution.py:297
  31.4 6.9 %collective-permute-start.1 = (f32[2,2,8,512]{3,2,1,0:T(8,128)S(1)}, f32[2,2,8,512]{3,2,1,0:T(8,128)S(1)}, u32[]{:S(2)}, u32[]{:S(2)}) collective-permute-start(f32[2,2,8,512]{3,2,1,0:T(8,128)S(1)} %get-tuple-element.21), channel_id=1, source_target_pairs={{0,2},{1,3},{2,0},{3,1},{4,6},{5,7},{6,4},{7,5},{16,18},{17,19},{1... | collective-permute-start | bytes 196616 | tf_op jit(solution)/shard_map/ppermute | solution.py:316
  33.3 9.9 %collective-permute-start.2 = (f32[2,2,8,512]{3,2,1,0:T(8,128)S(1)}, f32[2,2,8,512]{3,2,1,0:T(8,128)S(1)}, u32[]{:S(2)}, u32[]{:S(2)}) collective-permute-start(f32[2,2,8,512]{3,2,1,0:T(8,128)S(1)} %get-tuple-element.22), channel_id=1, source_target_pairs={{0,4},{1,5},{2,6},{3,7},{4,0},{5,1},{6,2},{7,3},{16,20},{17,21},{1... | collective-permute-start | bytes 196616 | tf_op jit(solution)/shard_map/ppermute | solution.py:316
  35.7 8.7 %collective-permute-start.3 = (f32[2,2,8,512]{3,2,1,0:T(8,128)S(1)}, f32[2,2,8,512]{3,2,1,0:T(8,128)S(1)}, u32[]{:S(2)}, u32[]{:S(2)}) collective-permute-start(f32[2,2,8,512]{3,2,1,0:T(8,128)S(1)} %get-tuple-element.23), channel_id=1, source_target_pairs={{0,6},{1,7},{2,4},{3,5},{4,2},{5,3},{6,0},{7,1},{16,22},{17,23},{1... | collective-permute-start | bytes 196616 | tf_op jit(solution)/shard_map/ppermute | solution.py:316
  35.8 8.5 %collective-permute-start.4 = (f32[2,2,8,512]{3,2,1,0:T(8,128)S(1)}, f32[2,2,8,512]{3,2,1,0:T(8,128)S(1)}, u32[]{:S(2)}, u32[]{:S(2)}) collective-permute-start(f32[2,2,8,512]{3,2,1,0:T(8,128)S(1)} %get-tuple-element.24), channel_id=1, source_target_pairs={{0,16},{1,17},{2,18},{3,19},{4,20},{5,21},{6,22},{7,23},{16,0},{17... | collective-permute-start | bytes 196616 | tf_op jit(solution)/shard_map/ppermute | solution.py:316
  36.7 7.6 %collective-permute-start.5 = (f32[2,2,8,512]{3,2,1,0:T(8,128)S(1)}, f32[2,2,8,512]{3,2,1,0:T(8,128)S(1)}, u32[]{:S(2)}, u32[]{:S(2)}) collective-permute-start(f32[2,2,8,512]{3,2,1,0:T(8,128)S(1)} %get-tuple-element.25), channel_id=1, source_target_pairs={{0,18},{1,19},{2,16},{3,17},{4,22},{5,23},{6,20},{7,21},{16,2},{17... | collective-permute-start | bytes 196616 | tf_op jit(solution)/shard_map/ppermute | solution.py:316
  38.3 9.8 %collective-permute-start.6 = (f32[2,2,8,512]{3,2,1,0:T(8,128)S(1)}, f32[2,2,8,512]{3,2,1,0:T(8,128)S(1)}, u32[]{:S(2)}, u32[]{:S(2)}) collective-permute-start(f32[2,2,8,512]{3,2,1,0:T(8,128)S(1)} %get-tuple-element.26), channel_id=1, source_target_pairs={{0,20},{1,21},{2,22},{3,23},{4,16},{5,17},{6,18},{7,19},{16,4},{17... | collective-permute-start | bytes 196616 | tf_op jit(solution)/shard_map/ppermute | solution.py:316
  43.2 7.0 %collective-permute-start.7 = (f32[2,2,8,512]{3,2,1,0:T(8,128)S(1)}, f32[2,2,8,512]{3,2,1,0:T(8,128)S(1)}, u32[]{:S(2)}, u32[]{:S(2)}) collective-permute-start(f32[2,2,8,512]{3,2,1,0:T(8,128)S(1)} %get-tuple-element.27), channel_id=1, source_target_pairs={{0,22},{1,23},{2,20},{3,21},{4,18},{5,19},{6,16},{7,17},{16,6},{17... | collective-permute-start | bytes 196616 | tf_op jit(solution)/shard_map/ppermute | solution.py:316
  52.0 13.1 %all-to-all-start = ((f32[8,2,8,512]{3,2,1,0:T(8,128)}), f32[8,2,8,512]{3,2,1,0:T(8,128)S(1)}, u32[]{:S(2)}, u32[]{:S(2)}) async-start(f32[8,2,8,512]{3,2,1,0:T(8,128)} %shard_map.68), calls=%async_computation | async-start | bytes 524288 | tf_op jit(solution)/shard_map/all_to_all | solution.py:349

commit v4 on v3

--- a/solution.py
+++ b/solution.py
@@ -178,6 +178,12 @@
         out[1] = got[t // chips, t % chips]
 
 
+def join_back_kernel(mine, got, *outs):
+    for z, out in enumerate(outs):
+        out[0] = mine[z]
+        out[1] = got[z]
+
+
 def correlate(got, forward, backward, twist, out, keep, halves, left, right):
     count = got.shape[0] // 2
     rows = got.shape[2]
@@ -218,7 +224,8 @@
 
 
 def correlate_pieces(pieces, *refs):
-    got, blocks, rest = refs[-1], refs[:pieces], refs[pieces:-1]
+    blocks, (forward, backward, twist, mine, give) = refs[:pieces], refs[pieces : pieces + 5]
+    got, out, *rest = refs[pieces + 5 :]
     chips = pieces // 2
     own = lax.axis_index("half")
     me = lax.axis_index("en")
@@ -226,7 +233,10 @@
         half = own if t < chips else 1 - own
         for core in range(2):
             got[half * (2 * chips) + (me ^ (2 * (t % chips) + core))] = block[core]
-    correlate(got, *rest)
+    correlate(got, forward, backward, twist, out, *rest)
+    for z in range(chips):
+        for core, target in enumerate((mine, give)):
+            target[z] = out[me ^ (2 * z + core)]
 
 
 def hold_kernel(block, out):
@@ -237,10 +247,25 @@
     return sorted(range(1, 2 * chips), key=lambda t: (-(t % chips), t < chips))
 
 
-def unpack_kernel(chunk, *refs):
-    returned, out, sems = refs[0], refs[-2], refs[-1]
+def keep_first_kernel(returned, out, sems):
     copies = [
-        pltpu.make_async_copy(returned.at[:, p], out.at[p, :, chunk], sems.at[p]) for p in range(2)
+        pltpu.make_async_copy(returned.at[:, p], out.at[p, :, 0], sems.at[p]) for p in range(2)
+    ]
+    for copy in copies:
+        copy.start()
+    for copy in copies:
+        copy.wait()
+
+
+def keep_second_kernel(*refs):
+    *bundles, _, out, sems = refs
+    me = lax.axis_index("en")
+    copies = [
+        pltpu.make_async_copy(
+            bundle.at[core], out.at[:, me ^ (2 * z + core), 1], sems.at[z, core]
+        )
+        for z, bundle in enumerate(bundles)
+        for core in range(2)
     ]
     for copy in copies:
         copy.start()
@@ -321,8 +346,6 @@
         jnp.asarray(twiddles(points)),
     )
     settings = dict(
-        out_shape=jax.ShapeDtypeStruct((count, *block), f32),
-        out_specs=in_vmem,
         compiler_params=pltpu.CompilerParams(vmem_limit_bytes=16 << 20),
         cost_estimate=pl.CostEstimate(
             flops=3 * 2 * 3 * points * SUBLANES * 4 * LANES * LANES,
@@ -336,31 +359,56 @@
         pltpu.VMEM((points * SUBLANES, 2 * LANES), f32),
         pltpu.VMEM((points * SUBLANES, 2 * LANES), f32),
     ]
-    result_a = pl.pallas_call(
-        correlate, in_specs=[in_vmem] * 4, scratch_shapes=scratch, **settings
+    result = pl.pallas_call(
+        correlate,
+        out_shape=jax.ShapeDtypeStruct((count, *block), f32),
+        in_specs=[in_vmem] * 4,
+        out_specs=in_vmem,
+        scratch_shapes=scratch,
+        **settings,
     )(got, *tables)
-    back_a = lax.all_to_all(result_a, "en", 0, 0, tiled=True)
-    result_b = pl.pallas_call(
+    returned = lax.all_to_all(result, "en", 0, 0, tiled=True)
+    mine, give = pl.pallas_call(
         functools.partial(correlate_pieces, 2 * chips),
+        out_shape=[jax.ShapeDtypeStruct((chips, *block), f32)] * 2,
         in_specs=[in_vmem] * (2 * chips + 3),
-        scratch_shapes=scratch + [pltpu.VMEM((2 * count, *block), f32)],
+        out_specs=[in_vmem] * 2,
+        scratch_shapes=[
+            pltpu.VMEM((2 * count, *block), f32),
+            pltpu.VMEM((count, *block), f32),
+            *scratch,
+        ],
         **settings,
     )(*arrived, *tables)
-    back_b = lax.all_to_all(result_b, "en", 0, 0, tiled=True)
-
-    def unpack(chunk, returned, *held):
-        return pl.pallas_call(
-            functools.partial(unpack_kernel, chunk),
-            out_shape=jax.ShapeDtypeStruct(tiled, f32),
-            in_specs=[in_vmem] + [in_hbm] * len(held),
-            out_specs=in_hbm,
-            scratch_shapes=[pltpu.SemaphoreType.DMA((2,))],
-            input_output_aliases={1: 0} if held else {},
-            compiler_params=pltpu.CompilerParams(vmem_limit_bytes=1 << 20),
-        )(returned, *held)
-
-    kept = unpack(0, back_a)
-    out = unpack(1, back_b, kept)
+    given = lax.ppermute(give, "en", [(e, e ^ 1) for e in range(count)])
+    bundles = pl.pallas_call(
+        join_back_kernel,
+        out_shape=[bundle] * chips,
+        in_specs=[in_vmem] * 2,
+        out_specs=[in_vmem] * chips,
+        compiler_params=pltpu.CompilerParams(vmem_limit_bytes=4 << 20),
+    )(mine, given)
+    bundles = list(bundles)
+    for z in range(chips - 1, 0, -1):
+        bundles[z] = lax.ppermute(bundles[z], "en", [(e, e ^ (2 * z)) for e in range(count)])
+    whole = jax.ShapeDtypeStruct(tiled, f32)
+    kept = pl.pallas_call(
+        keep_first_kernel,
+        out_shape=whole,
+        in_specs=[in_vmem],
+        out_specs=in_hbm,
+        scratch_shapes=[pltpu.SemaphoreType.DMA((2,))],
+        compiler_params=pltpu.CompilerParams(vmem_limit_bytes=1 << 20),
+    )(returned)
+    out = pl.pallas_call(
+        keep_second_kernel,
+        out_shape=whole,
+        in_specs=[in_vmem] * chips + [in_hbm],
+        out_specs=in_hbm,
+        scratch_shapes=[pltpu.SemaphoreType.DMA((chips, 2))],
+        input_output_aliases={chips: 0},
+        compiler_params=pltpu.CompilerParams(vmem_limit_bytes=1 << 20),
+    )(*bundles, kept)
     return out.reshape(2, group_rows, local_len)
 
 

time: 66.2 us -> 63.4 us (0.958)
  blocking collectives: 21.6 us -> 0 us
  waiting for transfers between devices: 17.5 us -> 27.9 us
  starting transfers between devices: 19.2 us -> 27.6 us
    all_to_all x1 -> x0, blocking collectives: 21.6 us -> none  [body(): got = lax.all_to_all(packed, ('half', 'en'), 0, 0, tiled=True)]
    ppermute x0 -> x3, starting transfers between devices: none -> 4.44 us  [body(): lax.ppermute(bundles[z], 'en', [(e, e ^ 2 * z) for e in range(count)])]
    all_to_all x2, starting transfers between devices: 7.29 us -> 11.3 us  [the longest x1 7.43 us: body(): got = lax.all_to_all(packed, ('half', 'en'), 0, 0, tiled=True)]
    all_to_all x2, waiting for transfers between devices: 8.91 us -> 12.7 us  [the longest x1 12.7 us: body(): got = lax.all_to_all(packed, ('half', 'en'), 0, 0, tiled=True)]
    ppermute x0 -> x3, waiting for transfers between devices: none -> 3.52 us  [body(): lax.ppermute(bundles[z], 'en', [(e, e ^ 2 * z) for e in range(count)])]
    ppermute x7, waiting for transfers between devices: 7.43 us -> 10.3 us  [body(): arrived[t] = lax.ppermute(bundles[t], ('half', 'en'), route)]
    pallas_call x4 -> x5, Pallas kernels: 4.98 us -> 4.36 us  [the longest x1 1.77 us: body(): pl.pallas_call(correlate, out_shape=jax.ShapeDtypeStruct((count, *block),...]
    ppermute x1 -> x2, waiting for transfers between devices: 1.16 us -> 1.34 us  [body(): given = lax.ppermute(give, 'en', [(e, e ^ 1) for e in range(count)])]
  transfers between devices with their start and end apart: 10 -> 14, of which waited for: 5 -> 7; matrix products, arithmetic and copies ran while one was open for 0% -> 0% of each run, Pallas kernels for 5% -> 7%
where the time goes in v4:
time: 63.4 us; the launch traced here: 63 us
  waiting for transfers between devices  27.9 us (44%)
  starting transfers between devices  27.6 us (44%)
  Pallas kernels  7.41 us (12%)
    all_to_all x1, waiting for transfers between devices, body(): got = lax.all_to_all(packed, ('half', 'en'), 0, 0, tiled=True)  12.7 us
    ppermute x7, starting transfers between devices, body(): arrived[t] = lax.ppermute(bundles[t], ('half', 'en'), route)  11.3 us
    ppermute x7, waiting for transfers between devices, body(): arrived[t] = lax.ppermute(bundles[t], ('half', 'en'), route)  10.3 us
    all_to_all x1, starting transfers between devices, body(): got = lax.all_to_all(packed, ('half', 'en'), 0, 0, tiled=True)  7.43 us
    ppermute x3, starting transfers between devices, body(): lax.ppermute(bundles[z], 'en', [(e, e ^ 2 * z) for e in range(count)])  4.44 us
    all_to_all x1, starting transfers between devices, body(): returned = lax.all_to_all(result, 'en', 0, 0, tiled=True)  3.88 us
    ppermute x3, waiting for transfers between devices, body(): lax.ppermute(bundles[z], 'en', [(e, e ^ 2 * z) for e in range(count)])  3.52 us
    pallas_call x1, Pallas kernels, body(): pl.pallas_call(pack_kernel, out_shape=[jax.ShapeDtypeStruct((2 * count, *...  2 us
  transfers between devices with their start and end apart: 14, of which 7 were waited for; matrix products, arithmetic and copies ran while one was open for 0% of the time, Pallas kernels for 7%

profile of v4, /device:TPU:0, one launch (start us, length us, event | category | flops | bytes accessed | tf_op | source)
XLA Modules:
  0.0 63.0 jit_solution(17202848131838249816)
XLA Ops:
  0.0 2.0 %shard_map.64 = (f32[16,2,8,512]{3,2,1,0:T(8,128)}, f32[8,2,8,512]{3,2,1,0:T(8,128)S(1)}) custom-call(s32[1,128]{1,0:T(1,128)} %bitcast.7, f32[2,8,2,8,512]{4,3,2,1,0:T(8,128)} %bitcast.4, f32[2,8,2,8,512]{4,3,2,1,0:T(8,128)} %bitcast.6), custom_call_target="tpu_custom_call" | custom-call | tf_op jit(solution)/shard_map/pallas_call | solution.py:297
  2.0 7.4 %all-to-all-start = ((f32[16,2,8,512]{3,2,1,0:T(8,128)}), f32[16,2,8,512]{3,2,1,0:T(8,128)S(1)}, u32[]{:S(2)}, u32[]{:S(2)}) async-start(f32[16,2,8,512]{3,2,1,0:T(8,128)} %get-tuple-element.40), calls=%async_computation | async-start | bytes 1048576 | tf_op jit(solution)/shard_map/all_to_all | solution.py:313
  9.4 0.0 copy-start
  9.5 0.0 copy-start.1
  9.5 0.0 copy-start.2
  9.5 1.0 %shard_map.65 = (f32[2,4,2,8,512]{4,3,2,1,0:T(8,128)S(1)}, f32[2,4,2,8,512]{4,3,2,1,0:T(8,128)S(1)}) custom-call(f32[2,8,2,8,512]{4,3,2,1,0:T(8,128)} %bitcast.5, f32[8,2,8,512]{3,2,1,0:T(8,128)S(1)} %get-tuple-element.23.second), custom_call_target="tpu_custom_call" | custom-call | tf_op jit(solution)/shard_map/pallas_call | solution.py:314
  10.5 0.5 collective-permute-start
  11.0 12.7 %all-to-all-done.got = f32[16,2,8,512]{3,2,1,0:T(8,128)S(1)} async-done(((f32[16,2,8,512]{3,2,1,0:T(8,128)}), f32[16,2,8,512]{3,2,1,0:T(8,128)S(1)}, u32[]{:S(2)}, u32[]{:S(2)}) %all-to-all-start) | async-done | bytes 524320 | tf_op jit(solution)/shard_map/all_to_all | solution.py:313
  23.7 0.0 copy-done
  23.7 0.0 copy-done.1
  23.7 0.0 copy-done.2
  23.7 1.8 %shard_map.70 = f32[8,2,8,512]{3,2,1,0:T(8,128)} custom-call(f32[16,2,8,512]{3,2,1,0:T(8,128)S(1)} %all-to-all-done.got, bf16[2,256,256]{2,1,0:T(8,128)(2,1)S(1)} %copy-done.1, bf16[2,256,256]{2,1,0:T(8,128)(2,1)S(1)} %copy-done, f32[2,32,128]{2,1,0:T(8,128)S(1)} %copy-done.2), custom_call_target="tpu_custom_call" | custom-call | flops 301989888 | bytes 4194304 | tf_op jit(solution)/shard_map/pallas_call | solution.py:362
  25.4 3.9 %all-to-all-start.1 = ((f32[8,2,8,512]{3,2,1,0:T(8,128)}), f32[8,2,8,512]{3,2,1,0:T(8,128)S(1)}, u32[]{:S(2)}, u32[]{:S(2)}) async-start(f32[8,2,8,512]{3,2,1,0:T(8,128)} %shard_map.70), calls=%async_computation.1 | async-start | bytes 524288 | tf_op jit(solution)/shard_map/all_to_all | solution.py:370
  29.3 0.0 collective-permute-done.got
  29.4 2.1 %collective-permute-start.1 = (f32[2,2,8,512]{3,2,1,0:T(8,128)S(1)}, f32[2,2,8,512]{3,2,1,0:T(8,128)S(1)}, u32[]{:S(2)}, u32[]{:S(2)}) collective-permute-start(f32[2,2,8,512]{3,2,1,0:T(8,128)S(1)} %get-tuple-element.27), channel_id=1, source_target_pairs={{0,2},{1,3},{2,0},{3,1},{4,6},{5,7},{6,4},{7,5},{16,18},{17,19},{1... | collective-permute-start | bytes 196616 | tf_op jit(solution)/shard_map/ppermute | solution.py:341
  31.5 2.4 %collective-permute-start.2 = (f32[2,2,8,512]{3,2,1,0:T(8,128)S(1)}, f32[2,2,8,512]{3,2,1,0:T(8,128)S(1)}, u32[]{:S(2)}, u32[]{:S(2)}) collective-permute-start(f32[2,2,8,512]{3,2,1,0:T(8,128)S(1)} %get-tuple-element.28), channel_id=1, source_target_pairs={{0,4},{1,5},{2,6},{3,7},{4,0},{5,1},{6,2},{7,3},{16,20},{17,21},{1... | collective-permute-start | bytes 196616 | tf_op jit(solution)/shard_map/ppermute | solution.py:341
  33.8 0.1 collective-permute-start.3
  33.9 0.7 %collective-permute-start.4 = (f32[2,2,8,512]{3,2,1,0:T(8,128)S(1)}, f32[2,2,8,512]{3,2,1,0:T(8,128)S(1)}, u32[]{:S(2)}, u32[]{:S(2)}) collective-permute-start(f32[2,2,8,512]{3,2,1,0:T(8,128)S(1)} %get-tuple-element.30), channel_id=1, source_target_pairs={{0,16},{1,17},{2,18},{3,19},{4,20},{5,21},{6,22},{7,23},{16,0},{17... | collective-permute-start | bytes 196616 | tf_op jit(solution)/shard_map/ppermute | solution.py:341
  34.6 1.8 %collective-permute-start.5 = (f32[2,2,8,512]{3,2,1,0:T(8,128)S(1)}, f32[2,2,8,512]{3,2,1,0:T(8,128)S(1)}, u32[]{:S(2)}, u32[]{:S(2)}) collective-permute-start(f32[2,2,8,512]{3,2,1,0:T(8,128)S(1)} %get-tuple-element.31), channel_id=1, source_target_pairs={{0,18},{1,19},{2,16},{3,17},{4,22},{5,23},{6,20},{7,21},{16,2},{17... | collective-permute-start | bytes 196616 | tf_op jit(solution)/shard_map/ppermute | solution.py:341
  36.4 1.4 %collective-permute-done.1.refs_1_ = f32[2,2,8,512]{3,2,1,0:T(8,128)S(1)} collective-permute-done((f32[2,2,8,512]{3,2,1,0:T(8,128)S(1)}, f32[2,2,8,512]{3,2,1,0:T(8,128)S(1)}, u32[]{:S(2)}, u32[]{:S(2)}) %collective-permute-start.1) | collective-permute-done | bytes 65568 | tf_op jit(solution)/shard_map/ppermute | solution.py:341
  37.8 3.4 %collective-permute-start.6 = (f32[2,2,8,512]{3,2,1,0:T(8,128)S(1)}, f32[2,2,8,512]{3,2,1,0:T(8,128)S(1)}, u32[]{:S(2)}, u32[]{:S(2)}) collective-permute-start(f32[2,2,8,512]{3,2,1,0:T(8,128)S(1)} %get-tuple-element.32), channel_id=1, source_target_pairs={{0,20},{1,21},{2,22},{3,23},{4,16},{5,17},{6,18},{7,19},{16,4},{17... | collective-permute-start | bytes 196616 | tf_op jit(solution)/shard_map/ppermute | solution.py:341
  41.2 2.9 %collective-permute-done.2.refs_2_ = f32[2,2,8,512]{3,2,1,0:T(8,128)S(1)} collective-permute-done((f32[2,2,8,512]{3,2,1,0:T(8,128)S(1)}, f32[2,2,8,512]{3,2,1,0:T(8,128)S(1)}, u32[]{:S(2)}, u32[]{:S(2)}) %collective-permute-start.2) | collective-permute-done | bytes 65568 | tf_op jit(solution)/shard_map/ppermute | solution.py:341
  44.1 0.9 %collective-permute-start.7 = (f32[2,2,8,512]{3,2,1,0:T(8,128)S(1)}, f32[2,2,8,512]{3,2,1,0:T(8,128)S(1)}, u32[]{:S(2)}, u32[]{:S(2)}) collective-permute-start(f32[2,2,8,512]{3,2,1,0:T(8,128)S(1)} %get-tuple-element.33), channel_id=1, source_target_pairs={{0,22},{1,23},{2,20},{3,21},{4,18},{5,19},{6,16},{7,17},{16,6},{17... | collective-permute-start | bytes 196616 | tf_op jit(solution)/shard_map/ppermute | solution.py:341
  45.0 0.0 collective-permute-done.3.refs_3_
  45.0 0.0 collective-permute-done.4.refs_4_
  45.0 0.0 collective-permute-done.5.refs_5_
  45.0 3.8 %collective-permute-done.6.refs_6_ = f32[2,2,8,512]{3,2,1,0:T(8,128)S(1)} collective-permute-done((f32[2,2,8,512]{3,2,1,0:T(8,128)S(1)}, f32[2,2,8,512]{3,2,1,0:T(8,128)S(1)}, u32[]{:S(2)}, u32[]{:S(2)}) %collective-permute-start.6) | collective-permute-done | bytes 65568 | tf_op jit(solution)/shard_map/ppermute | solution.py:341
  48.8 2.2 %collective-permute-done.7.refs_7_ = f32[2,2,8,512]{3,2,1,0:T(8,128)S(1)} collective-permute-done((f32[2,2,8,512]{3,2,1,0:T(8,128)S(1)}, f32[2,2,8,512]{3,2,1,0:T(8,128)S(1)}, u32[]{:S(2)}, u32[]{:S(2)}) %collective-permute-start.7) | collective-permute-done | bytes 65568 | tf_op jit(solution)/shard_map/ppermute | solution.py:341
  51.0 1.1 %shard_map.68 = (f32[4,2,8,512]{3,2,1,0:T(8,128)S(1)}, f32[4,2,8,512]{3,2,1,0:T(8,128)S(1)}) custom-call(f32[2,2,8,512]{3,2,1,0:T(8,128)S(1)} %shard_map.67.refs_0_, f32[2,2,8,512]{3,2,1,0:T(8,128)S(1)} %collective-permute-done.1.refs_1_, f32[2,2,8,512]{3,2,1,0:T(8,128)S(1)} %collective-permute-done.2.refs_2_, ...), custom_call_target="tpu_custom_call" | custom-call | flops 301989888 | bytes 4194304 | tf_op jit(solution)/shard_map/pallas_call | solution.py:371
  52.1 0.1 collective-permute-start.8
  52.2 1.3 %collective-permute-done.8.got = f32[4,2,8,512]{3,2,1,0:T(8,128)S(1)} collective-permute-done((f32[4,2,8,512]{3,2,1,0:T(8,128)S(1)}, f32[4,2,8,512]{3,2,1,0:T(8,128)S(1)}, u32[]{:S(2)}, u32[]{:S(2)}) %collective-permute-start.8) | collective-permute-done | bytes 131104 | tf_op jit(solution)/shard_map/ppermute | solution.py:383
  53.6 0.1 collective-permute-start.9
  53.7 1.2 %collective-permute-start.10 = (f32[2,2,8,512]{3,2,1,0:T(8,128)S(1)}, f32[2,2,8,512]{3,2,1,0:T(8,128)S(1)}, u32[]{:S(2)}, u32[]{:S(2)}) collective-permute-start(f32[2,2,8,512]{3,2,1,0:T(8,128)S(1)} %get-tuple-element.38), channel_id=1, source_target_pairs={{0,4},{1,5},{2,6},{3,7},{4,0},{5,1},{6,2},{7,3},{8,12},{9,13},{10,... | collective-permute-start | bytes 196616 | tf_op jit(solution)/shard_map/ppermute | solution.py:393
  54.8 3.2 %collective-permute-start.11 = (f32[2,2,8,512]{3,2,1,0:T(8,128)S(1)}, f32[2,2,8,512]{3,2,1,0:T(8,128)S(1)}, u32[]{:S(2)}, u32[]{:S(2)}) collective-permute-start(f32[2,2,8,512]{3,2,1,0:T(8,128)S(1)} %get-tuple-element.39), channel_id=1, source_target_pairs={{0,6},{1,7},{2,4},{3,5},{4,2},{5,3},{6,0},{7,1},{8,14},{9,15},{10,... | collective-permute-start | bytes 196616 | tf_op jit(solution)/shard_map/ppermute | solution.py:393
  58.0 0.0 all-to-all-done.1.returned
  58.0 0.7 %shard_map.71.refs_4_ = f32[2,8,2,8,512]{4,3,2,1,0:T(8,128)} custom-call(f32[8,2,8,512]{3,2,1,0:T(8,128)S(1)} %all-to-all-done.1.returned), custom_call_target="tpu_custom_call" | custom-call | tf_op jit(solution)/shard_map/pallas_call | solution.py:395
  58.8 0.0 collective-permute-done.9.refs_1_
  58.8 3.5 %collective-permute-done.10.refs_2_ = f32[2,2,8,512]{3,2,1,0:T(8,128)S(1)} collective-permute-done((f32[2,2,8,512]{3,2,1,0:T(8,128)S(1)}, f32[2,2,8,512]{3,2,1,0:T(8,128)S(1)}, u32[]{:S(2)}, u32[]{:S(2)}) %collective-permute-start.10) | collective-permute-done | bytes 65568 | tf_op jit(solution)/shard_map/ppermute | solution.py:393
  62.3 0.0 collective-permute-done.11.refs_3_
  62.3 0.8 %shard_map.72 = f32[2,8,2,8,512]{4,3,2,1,0:T(8,128)} custom-call(f32[2,2,8,512]{3,2,1,0:T(8,128)S(1)} %get-tuple-element.36.refs_0_, f32[2,2,8,512]{3,2,1,0:T(8,128)S(1)} %collective-permute-done.9.refs_1_, f32[2,2,8,512]{3,2,1,0:T(8,128)S(1)} %collective-permute-done.10.refs_2_, ...), custom_call_target="tpu_custom_call", output_to_operand_aliasing={{}: (4, {})} | custom-call | tf_op jit(solution)/shard_map/pallas_call | solution.py:403
  (3 shorter events, 0.1 us)
Async XLA Ops:
  2.0 21.7 %all-to-all-start = ((f32[16,2,8,512]{3,2,1,0:T(8,128)}), f32[16,2,8,512]{3,2,1,0:T(8,128)S(1)}, u32[]{:S(2)}, u32[]{:S(2)}) async-start(f32[16,2,8,512]{3,2,1,0:T(8,128)} %get-tuple-element.40), calls=%async_computation | async-start | bytes 1048576 | tf_op jit(solution)/shard_map/all_to_all | solution.py:313
  9.4 14.2 %copy-start = (bf16[2,256,256]{2,1,0:T(8,128)(2,1)S(1)}, bf16[2,256,256]{2,1,0:T(8,128)(2,1)}, u32[]{:S(2)}) copy-start(bf16[2,256,256]{2,1,0:T(8,128)(2,1)} %constant.7.clone.refs_9_.backward) | copy-start | bytes 786436
  9.5 14.2 %copy-start.1 = (bf16[2,256,256]{2,1,0:T(8,128)(2,1)S(1)}, bf16[2,256,256]{2,1,0:T(8,128)(2,1)}, u32[]{:S(2)}) copy-start(bf16[2,256,256]{2,1,0:T(8,128)(2,1)} %constant.6.clone.refs_8_.forward) | copy-start | bytes 786436
  9.5 14.2 %copy-start.2 = (f32[2,32,128]{2,1,0:T(8,128)S(1)}, f32[2,32,128]{2,1,0:T(8,128)}, u32[]{:S(2)}) copy-start(f32[2,32,128]{2,1,0:T(8,128)} %constant.8.clone.refs_10_.twist) | copy-start | bytes 98308
  10.5 18.8 %collective-permute-start = (f32[2,4,2,8,512]{4,3,2,1,0:T(8,128)S(1)}, f32[2,4,2,8,512]{4,3,2,1,0:T(8,128)S(1)}, u32[]{:S(2)}, u32[]{:S(2)}) collective-permute-start(f32[2,4,2,8,512]{4,3,2,1,0:T(8,128)S(1)} %get-tuple-element.25), channel_id=1, source_target_pairs={{0,1},{1,0},{2,3},{3,2},{4,5},{5,4},{6,7},{7,6},{8,9},{9,8},{10,11... | collective-permute-start | bytes 786440 | tf_op jit(solution)/shard_map/ppermute | solution.py:322
  25.4 32.6 %all-to-all-start.1 = ((f32[8,2,8,512]{3,2,1,0:T(8,128)}), f32[8,2,8,512]{3,2,1,0:T(8,128)S(1)}, u32[]{:S(2)}, u32[]{:S(2)}) async-start(f32[8,2,8,512]{3,2,1,0:T(8,128)} %shard_map.70), calls=%async_computation.1 | async-start | bytes 524288 | tf_op jit(solution)/shard_map/all_to_all | solution.py:370
  29.4 8.4 %collective-permute-start.1 = (f32[2,2,8,512]{3,2,1,0:T(8,128)S(1)}, f32[2,2,8,512]{3,2,1,0:T(8,128)S(1)}, u32[]{:S(2)}, u32[]{:S(2)}) collective-permute-start(f32[2,2,8,512]{3,2,1,0:T(8,128)S(1)} %get-tuple-element.27), channel_id=1, source_target_pairs={{0,2},{1,3},{2,0},{3,1},{4,6},{5,7},{6,4},{7,5},{16,18},{17,19},{1... | collective-permute-start | bytes 196616 | tf_op jit(solution)/shard_map/ppermute | solution.py:341
  31.5 12.6 %collective-permute-start.2 = (f32[2,2,8,512]{3,2,1,0:T(8,128)S(1)}, f32[2,2,8,512]{3,2,1,0:T(8,128)S(1)}, u32[]{:S(2)}, u32[]{:S(2)}) collective-permute-start(f32[2,2,8,512]{3,2,1,0:T(8,128)S(1)} %get-tuple-element.28), channel_id=1, source_target_pairs={{0,4},{1,5},{2,6},{3,7},{4,0},{5,1},{6,2},{7,3},{16,20},{17,21},{1... | collective-permute-start | bytes 196616 | tf_op jit(solution)/shard_map/ppermute | solution.py:341
  33.8 11.2 %collective-permute-start.3 = (f32[2,2,8,512]{3,2,1,0:T(8,128)S(1)}, f32[2,2,8,512]{3,2,1,0:T(8,128)S(1)}, u32[]{:S(2)}, u32[]{:S(2)}) collective-permute-start(f32[2,2,8,512]{3,2,1,0:T(8,128)S(1)} %get-tuple-element.29), channel_id=1, source_target_pairs={{0,6},{1,7},{2,4},{3,5},{4,2},{5,3},{6,0},{7,1},{16,22},{17,23},{1... | collective-permute-start | bytes 196616 | tf_op jit(solution)/shard_map/ppermute | solution.py:341
  33.9 11.1 %collective-permute-start.4 = (f32[2,2,8,512]{3,2,1,0:T(8,128)S(1)}, f32[2,2,8,512]{3,2,1,0:T(8,128)S(1)}, u32[]{:S(2)}, u32[]{:S(2)}) collective-permute-start(f32[2,2,8,512]{3,2,1,0:T(8,128)S(1)} %get-tuple-element.30), channel_id=1, source_target_pairs={{0,16},{1,17},{2,18},{3,19},{4,20},{5,21},{6,22},{7,23},{16,0},{17... | collective-permute-start | bytes 196616 | tf_op jit(solution)/shard_map/ppermute | solution.py:341
  34.6 10.4 %collective-permute-start.5 = (f32[2,2,8,512]{3,2,1,0:T(8,128)S(1)}, f32[2,2,8,512]{3,2,1,0:T(8,128)S(1)}, u32[]{:S(2)}, u32[]{:S(2)}) collective-permute-start(f32[2,2,8,512]{3,2,1,0:T(8,128)S(1)} %get-tuple-element.31), channel_id=1, source_target_pairs={{0,18},{1,19},{2,16},{3,17},{4,22},{5,23},{6,20},{7,21},{16,2},{17... | collective-permute-start | bytes 196616 | tf_op jit(solution)/shard_map/ppermute | solution.py:341
  37.8 11.0 %collective-permute-start.6 = (f32[2,2,8,512]{3,2,1,0:T(8,128)S(1)}, f32[2,2,8,512]{3,2,1,0:T(8,128)S(1)}, u32[]{:S(2)}, u32[]{:S(2)}) collective-permute-start(f32[2,2,8,512]{3,2,1,0:T(8,128)S(1)} %get-tuple-element.32), channel_id=1, source_target_pairs={{0,20},{1,21},{2,22},{3,23},{4,16},{5,17},{6,18},{7,19},{16,4},{17... | collective-permute-start | bytes 196616 | tf_op jit(solution)/shard_map/ppermute | solution.py:341
  44.1 7.0 %collective-permute-start.7 = (f32[2,2,8,512]{3,2,1,0:T(8,128)S(1)}, f32[2,2,8,512]{3,2,1,0:T(8,128)S(1)}, u32[]{:S(2)}, u32[]{:S(2)}) collective-permute-start(f32[2,2,8,512]{3,2,1,0:T(8,128)S(1)} %get-tuple-element.33), channel_id=1, source_target_pairs={{0,22},{1,23},{2,20},{3,21},{4,18},{5,19},{6,16},{7,17},{16,6},{17... | collective-permute-start | bytes 196616 | tf_op jit(solution)/shard_map/ppermute | solution.py:341
  52.1 1.4 %collective-permute-start.8 = (f32[4,2,8,512]{3,2,1,0:T(8,128)S(1)}, f32[4,2,8,512]{3,2,1,0:T(8,128)S(1)}, u32[]{:S(2)}, u32[]{:S(2)}) collective-permute-start(f32[4,2,8,512]{3,2,1,0:T(8,128)S(1)} %get-tuple-element.35), channel_id=1, source_target_pairs={{0,1},{1,0},{2,3},{3,2},{4,5},{5,4},{6,7},{7,6},{8,9},{9,8},{10,11... | collective-permute-start | bytes 393224 | tf_op jit(solution)/shard_map/ppermute | solution.py:383
  53.6 5.2 %collective-permute-start.9 = (f32[2,2,8,512]{3,2,1,0:T(8,128)S(1)}, f32[2,2,8,512]{3,2,1,0:T(8,128)S(1)}, u32[]{:S(2)}, u32[]{:S(2)}) collective-permute-start(f32[2,2,8,512]{3,2,1,0:T(8,128)S(1)} %get-tuple-element.37), channel_id=1, source_target_pairs={{0,2},{1,3},{2,0},{3,1},{4,6},{5,7},{6,4},{7,5},{8,10},{9,11},{10,... | collective-permute-start | bytes 196616 | tf_op jit(solution)/shard_map/ppermute | solution.py:393
  53.7 8.6 %collective-permute-start.10 = (f32[2,2,8,512]{3,2,1,0:T(8,128)S(1)}, f32[2,2,8,512]{3,2,1,0:T(8,128)S(1)}, u32[]{:S(2)}, u32[]{:S(2)}) collective-permute-start(f32[2,2,8,512]{3,2,1,0:T(8,128)S(1)} %get-tuple-element.38), channel_id=1, source_target_pairs={{0,4},{1,5},{2,6},{3,7},{4,0},{5,1},{6,2},{7,3},{8,12},{9,13},{10,... | collective-permute-start | bytes 196616 | tf_op jit(solution)/shard_map/ppermute | solution.py:393
  54.8 7.4 %collective-permute-start.11 = (f32[2,2,8,512]{3,2,1,0:T(8,128)S(1)}, f32[2,2,8,512]{3,2,1,0:T(8,128)S(1)}, u32[]{:S(2)}, u32[]{:S(2)}) collective-permute-start(f32[2,2,8,512]{3,2,1,0:T(8,128)S(1)} %get-tuple-element.39), channel_id=1, source_target_pairs={{0,6},{1,7},{2,4},{3,5},{4,2},{5,3},{6,0},{7,1},{8,14},{9,15},{10,... | collective-permute-start | bytes 196616 | tf_op jit(solution)/shard_map/ppermute | solution.py:393

commit v5 on v3

--- a/solution.py
+++ b/solution.py
@@ -102,22 +102,22 @@
     return re * cos - im * sin, re * sin + im * cos
 
 
-def pack_kernel(mirror, lesser, greater, packed, second, places, held, ready, sems):
+def pack_kernel(mirror, lesser, greater, mine, give, second, places, held, first, sems, block_sems):
     _, count, tiles, sub, local_len = lesser.shape
     rows = tiles * sub
-    own = lax.axis_index("half")
+    chips = count // 2
+    me = lax.axis_index("en")
     loads = [pltpu.make_async_copy(mirror, places, sems.at[0])]
     loads += [pltpu.make_async_copy(greater.at[p], held.at[p], sems.at[1 + p]) for p in range(2)]
-    firsts = [
-        pltpu.make_async_copy(lesser.at[p, :, 0], ready.at[0, :, p], sems.at[3 + p])
-        for p in range(2)
-    ]
-    for copy in loads + firsts:
+    blocks = [
+        pltpu.make_async_copy(
+            lesser.at[:, me ^ (2 * z + core), 0], target.at[0, z], block_sems.at[core, z]
+        )
+        for z in range(chips)
+        for core, target in enumerate((mine, give))
+    ]
+    for copy in loads + blocks:
         copy.start()
-    stores = [
-        pltpu.make_async_copy(ready.at[0], packed.at[pl.ds(own * count, count)], sems.at[5]),
-        pltpu.make_async_copy(ready.at[1], packed.at[pl.ds((1 - own) * count, count)], sems.at[6]),
-    ]
     loads[0].wait()
     lane = lax.broadcasted_iota(jnp.int32, (rows, count * rows), 1)
     line = lax.broadcasted_iota(jnp.int32, (rows, count * rows), 0)
@@ -127,9 +127,6 @@
         jnp.sum(jnp.where(lane // rows == to, source, 0.0), axis=1, keepdims=True).astype(jnp.int32)
         for to in range(count)
     ]
-    for copy in firsts:
-        copy.wait()
-    stores[0].start()
     for part in range(2):
         loads[1 + part].wait()
         for to in range(count):
@@ -144,30 +141,32 @@
                         picked = jnp.take_along_axis(tile, wanted % sub, axis=0)
                         moved = jnp.where(wanted // sub == u, picked, moved)
                     if t == 0:
-                        ready[1, to, part, :, span] = moved
+                        first[to, part, :, span] = moved
                     else:
                         second[to, part, :, span] = moved
+    for z in range(chips):
+        for core, target in enumerate((mine, give)):
+            target[1, z] = first[me ^ (2 * z + core)]
+    for copy in blocks:
+        copy.wait()
+
+
+def pack_second_kernel(lesser, second, packed, ready, sems):
+    count = second.shape[0]
+    own = lax.axis_index("half")
+    loads = [
+        pltpu.make_async_copy(lesser.at[p, :, 1], ready.at[:, p], sems.at[p]) for p in range(2)
+    ]
+    stores = [
+        pltpu.make_async_copy(second, packed.at[pl.ds((1 - own) * count, count)], sems.at[2]),
+        pltpu.make_async_copy(ready, packed.at[pl.ds(own * count, count)], sems.at[3]),
+    ]
+    for copy in [*loads, stores[0]]:
+        copy.start()
+    for copy in loads:
+        copy.wait()
     stores[1].start()
     for copy in stores:
-        copy.wait()
-
-
-def split_kernel(lesser, second, mine, give, sems):
-    chips = mine.shape[1]
-    me = lax.axis_index("en")
-    copies = []
-    for z in range(chips):
-        for core, target in enumerate((mine, give)):
-            to = me ^ (2 * z + core)
-            copies.append(
-                pltpu.make_async_copy(lesser.at[:, to, 1], target.at[0, z], sems.at[core, z])
-            )
-    for copy in copies:
-        copy.start()
-    for z in range(chips):
-        for core, target in enumerate((mine, give)):
-            target[1, z] = second[me ^ (2 * z + core)]
-    for copy in copies:
         copy.wait()
 
 
@@ -176,6 +175,12 @@
     for t, out in enumerate(outs):
         out[0] = mine[t // chips, t % chips]
         out[1] = got[t // chips, t % chips]
+
+
+def join_back_kernel(mine, got, *outs):
+    for z, out in enumerate(outs):
+        out[0] = mine[z]
+        out[1] = got[z]
 
 
 def correlate(got, forward, backward, twist, out, keep, halves, left, right):
@@ -217,8 +222,21 @@
         out[t // steps, 1, :, where] = -c_re
 
 
+def send_back(out, mine, give):
+    me = lax.axis_index("en")
+    for z in range(mine.shape[0]):
+        for core, target in enumerate((mine, give)):
+            target[z] = out[me ^ (2 * z + core)]
+
+
+def correlate_whole(got, forward, backward, twist, mine, give, out, *rest):
+    correlate(got, forward, backward, twist, out, *rest)
+    send_back(out, mine, give)
+
+
 def correlate_pieces(pieces, *refs):
-    got, blocks, rest = refs[-1], refs[:pieces], refs[pieces:-1]
+    blocks, (forward, backward, twist, mine, give) = refs[:pieces], refs[pieces : pieces + 5]
+    got, out, *rest = refs[pieces + 5 :]
     chips = pieces // 2
     own = lax.axis_index("half")
     me = lax.axis_index("en")
@@ -226,7 +244,8 @@
         half = own if t < chips else 1 - own
         for core in range(2):
             got[half * (2 * chips) + (me ^ (2 * (t % chips) + core))] = block[core]
-    correlate(got, *rest)
+    correlate(got, forward, backward, twist, out, *rest)
+    send_back(out, mine, give)
 
 
 def hold_kernel(block, out):
@@ -237,10 +256,15 @@
     return sorted(range(1, 2 * chips), key=lambda t: (-(t % chips), t < chips))
 
 
-def unpack_kernel(chunk, *refs):
-    returned, out, sems = refs[0], refs[-2], refs[-1]
+def keep_kernel(chunk, chips, *refs):
+    bundles, out, sems = refs[:chips], refs[-2], refs[-1]
+    me = lax.axis_index("en")
     copies = [
-        pltpu.make_async_copy(returned.at[:, p], out.at[p, :, chunk], sems.at[p]) for p in range(2)
+        pltpu.make_async_copy(
+            bundle.at[core], out.at[:, me ^ (2 * z + core), chunk], sems.at[z, core]
+        )
+        for z, bundle in enumerate(bundles)
+        for core in range(2)
     ]
     for copy in copies:
         copy.start()
@@ -269,51 +293,52 @@
         pltpu.with_memory_space_constraint(x, pltpu.HBM)
         for x in (mirror[None], lesser.reshape(tiled), greater.reshape(tiled))
     )
-    packed, second = pl.pallas_call(
+    mine, give, second = pl.pallas_call(
         pack_kernel,
         out_shape=[
-            jax.ShapeDtypeStruct((2 * count, *block), f32),
+            jax.ShapeDtypeStruct(half_view, f32),
+            jax.ShapeDtypeStruct(half_view, f32),
             jax.ShapeDtypeStruct((count, *block), f32),
         ],
         in_specs=[in_hbm] * 3,
-        out_specs=[in_hbm, in_vmem],
+        out_specs=[in_vmem] * 3,
         scratch_shapes=[
             pltpu.VMEM((1, group_rows), jnp.int32),
             pltpu.VMEM(tiled, f32),
-            pltpu.VMEM((2, count, *block), f32),
-            pltpu.SemaphoreType.DMA((7,)),
+            pltpu.VMEM((count, *block), f32),
+            pltpu.SemaphoreType.DMA((3,)),
+            pltpu.SemaphoreType.DMA((2, chips)),
         ],
         compiler_params=pltpu.CompilerParams(vmem_limit_bytes=8 << 20),
     )(mirror, lesser, greater)
-    got = lax.all_to_all(packed, ("half", "en"), 0, 0, tiled=True)
-    mine, give = pl.pallas_call(
-        split_kernel,
-        out_shape=[jax.ShapeDtypeStruct(half_view, f32)] * 2,
+    swap = [(e, e ^ 1) for e in range(count)]
+
+    def join(kernel, mine, given, pieces):
+        return list(
+            pl.pallas_call(
+                kernel,
+                out_shape=[bundle] * pieces,
+                in_specs=[in_vmem] * 2,
+                out_specs=[in_vmem] * pieces,
+                compiler_params=pltpu.CompilerParams(vmem_limit_bytes=4 << 20),
+            )(mine, given)
+        )
+
+    given = lax.ppermute(give, "en", swap)
+    packed = pl.pallas_call(
+        pack_second_kernel,
+        out_shape=jax.ShapeDtypeStruct((2 * count, *block), f32),
         in_specs=[in_hbm, in_vmem],
-        out_specs=[in_vmem] * 2,
-        scratch_shapes=[pltpu.SemaphoreType.DMA((2, chips))],
+        out_specs=in_hbm,
+        scratch_shapes=[pltpu.VMEM((count, *block), f32), pltpu.SemaphoreType.DMA((4,))],
         compiler_params=pltpu.CompilerParams(vmem_limit_bytes=4 << 20),
     )(lesser, second)
-    given = lax.ppermute(give, "en", [(e, e ^ 1) for e in range(count)])
-    bundles = pl.pallas_call(
-        join_kernel,
-        out_shape=[bundle] * (2 * chips),
-        in_specs=[in_vmem] * 2,
-        out_specs=[in_vmem] * (2 * chips),
-        compiler_params=pltpu.CompilerParams(vmem_limit_bytes=4 << 20),
-    )(mine, given)
-    arrived = list(bundles)
-    arrived[0] = pl.pallas_call(
-        hold_kernel,
-        out_shape=bundle,
-        in_specs=[in_vmem],
-        out_specs=in_vmem,
-        compiler_params=pltpu.CompilerParams(vmem_limit_bytes=1 << 20),
-    )(bundles[0])
+    arrived = join(join_kernel, mine, given, 2 * chips)
     for t in far_first(chips):
         step = t // chips * count + 2 * (t % chips)
         route = [(d, d ^ step) for d in range(2 * count)]
-        arrived[t] = lax.ppermute(bundles[t], ("half", "en"), route)
+        arrived[t] = lax.ppermute(arrived[t], ("half", "en"), route)
+    got = lax.all_to_all(packed, ("half", "en"), 0, 0, tiled=True)
 
     tables = (
         jnp.asarray(dft_block(1.0)),
@@ -321,8 +346,6 @@
         jnp.asarray(twiddles(points)),
     )
     settings = dict(
-        out_shape=jax.ShapeDtypeStruct((count, *block), f32),
-        out_specs=in_vmem,
         compiler_params=pltpu.CompilerParams(vmem_limit_bytes=16 << 20),
         cost_estimate=pl.CostEstimate(
             flops=3 * 2 * 3 * points * SUBLANES * 4 * LANES * LANES,
@@ -336,32 +359,54 @@
         pltpu.VMEM((points * SUBLANES, 2 * LANES), f32),
         pltpu.VMEM((points * SUBLANES, 2 * LANES), f32),
     ]
-    result_a = pl.pallas_call(
-        correlate, in_specs=[in_vmem] * 4, scratch_shapes=scratch, **settings
-    )(got, *tables)
-    back_a = lax.all_to_all(result_a, "en", 0, 0, tiled=True)
-    result_b = pl.pallas_call(
+    piece = jax.ShapeDtypeStruct((chips, *block), f32)
+    first = pl.pallas_call(
         functools.partial(correlate_pieces, 2 * chips),
+        out_shape=[piece] * 2,
         in_specs=[in_vmem] * (2 * chips + 3),
-        scratch_shapes=scratch + [pltpu.VMEM((2 * count, *block), f32)],
+        out_specs=[in_vmem] * 2,
+        scratch_shapes=[
+            pltpu.VMEM((2 * count, *block), f32),
+            pltpu.VMEM((count, *block), f32),
+            *scratch,
+        ],
         **settings,
     )(*arrived, *tables)
-    back_b = lax.all_to_all(result_b, "en", 0, 0, tiled=True)
-
-    def unpack(chunk, returned, *held):
-        return pl.pallas_call(
-            functools.partial(unpack_kernel, chunk),
-            out_shape=jax.ShapeDtypeStruct(tiled, f32),
-            in_specs=[in_vmem] + [in_hbm] * len(held),
-            out_specs=in_hbm,
-            scratch_shapes=[pltpu.SemaphoreType.DMA((2,))],
-            input_output_aliases={1: 0} if held else {},
-            compiler_params=pltpu.CompilerParams(vmem_limit_bytes=1 << 20),
-        )(returned, *held)
-
-    kept = unpack(0, back_a)
-    out = unpack(1, back_b, kept)
-    return out.reshape(2, group_rows, local_len)
+    second = pl.pallas_call(
+        correlate_whole,
+        out_shape=[piece] * 2,
+        in_specs=[in_vmem] * 4,
+        out_specs=[in_vmem] * 2,
+        scratch_shapes=[pltpu.VMEM((count, *block), f32), *scratch],
+        **settings,
+    )(got, *tables)
+    out = []
+    for chunk, (name, (mine, give)) in enumerate({"a": first, "b": second}.items()):
+        given = lax.ppermute(give, "en", swap)
+        bundles = join(join_back_kernel, mine, given, chips)
+        for z in range(chips - 1, 0, -1):
+            route = [(e, e ^ (2 * z)) for e in range(count)]
+            bundles[z] = lax.ppermute(bundles[z], "en", route)
+        if name == "a":
+            bundles[0] = pl.pallas_call(
+                hold_kernel,
+                out_shape=bundle,
+                in_specs=[in_vmem],
+                out_specs=in_vmem,
+                compiler_params=pltpu.CompilerParams(vmem_limit_bytes=1 << 20),
+            )(bundles[0])
+        out = [
+            pl.pallas_call(
+                functools.partial(keep_kernel, chunk, chips),
+                out_shape=jax.ShapeDtypeStruct(tiled, f32),
+                in_specs=[in_vmem] * chips + [in_hbm] * len(out),
+                out_specs=in_hbm,
+                scratch_shapes=[pltpu.SemaphoreType.DMA((chips, 2))],
+                input_output_aliases={chips: 0} if out else {},
+                compiler_params=pltpu.CompilerParams(vmem_limit_bytes=1 << 20),
+            )(*bundles, *out)
+        ]
+    return out[0].reshape(2, group_rows, local_len)
 
 
 def solution(mesh):

time: 66.2 us -> 57.1 us (0.86)
  blocking collectives: 21.6 us -> 0 us
  starting transfers between devices: 19.2 us -> 31.2 us
  waiting for transfers between devices: 17.5 us -> 18.6 us
    all_to_all x1 -> x0, blocking collectives: 21.6 us -> none  [body(): got = lax.all_to_all(packed, ('half', 'en'), 0, 0, tiled=True)]
    ppermute x8 -> x16, starting transfers between devices: 11.9 us -> 23.8 us  [the longest x7 13.8 us: body(): arrived[t] = lax.ppermute(arrived[t], ('half', 'en'), route)]
    ppermute x8 -> x16, waiting for transfers between devices: 8.6 us -> 18.6 us  [the longest x7 12.8 us: body(): arrived[t] = lax.ppermute(arrived[t], ('half', 'en'), route)]
    all_to_all x2 -> x1, waiting for transfers between devices: 8.91 us -> 0.01 us  [body(): got = lax.all_to_all(packed, ('half', 'en'), 0, 0, tiled=True)]
    pallas_call x7 -> x9, Pallas kernels: 7.31 us -> 6.93 us  [the longest x1 1.8 us: body(): pl.pallas_call(pack_second_kernel, out_shape=jax.ShapeDtypeStruct((2 * co...]
    all_to_all x2 -> x1, starting transfers between devices: 7.29 us -> 7.43 us  [body(): got = lax.all_to_all(packed, ('half', 'en'), 0, 0, tiled=True)]
  transfers between devices with their start and end apart: 10 -> 17, of which waited for: 5 -> 7; matrix products, arithmetic and copies ran while one was open for 0% -> 0% of each run, Pallas kernels for 5% -> 5%
where the time goes in v5:
time: 57.1 us; the launch traced here: 56.8 us
  starting transfers between devices  31.2 us (55%)
  waiting for transfers between devices  18.6 us (33%)
  Pallas kernels  6.93 us (12%)
    ppermute x7, starting transfers between devices, body(): arrived[t] = lax.ppermute(arrived[t], ('half', 'en'), route)  13.8 us
    ppermute x7, waiting for transfers between devices, body(): arrived[t] = lax.ppermute(arrived[t], ('half', 'en'), route)  12.8 us
    ppermute x6, starting transfers between devices, body(): bundles[z] = lax.ppermute(bundles[z], 'en', route)  8.89 us
    all_to_all x1, starting transfers between devices, body(): got = lax.all_to_all(packed, ('half', 'en'), 0, 0, tiled=True)  7.43 us
    ppermute x6, waiting for transfers between devices, body(): bundles[z] = lax.ppermute(bundles[z], 'en', route)  4.48 us
    pallas_call x1, Pallas kernels, body(): pl.pallas_call(pack_second_kernel, out_shape=jax.ShapeDtypeStruct((2 * co...  1.8 us
    pallas_call x2, Pallas kernels, body(): pl.pallas_call(functools.partial(keep_kernel, chunk, chips), out_shape=ja...  1.52 us
    pallas_call x1, Pallas kernels, body(): pl.pallas_call(pack_kernel, out_shape=[jax.ShapeDtypeStruct(half_view, f3...  1.35 us
  transfers between devices with their start and end apart: 17, of which 7 were waited for; matrix products, arithmetic and copies ran while one was open for 0% of the time, Pallas kernels for 5%

profile of v5, /device:TPU:0, one launch (start us, length us, event | category | flops | bytes accessed | tf_op | source)
XLA Modules:
  0.0 56.8 jit_solution(9135109835549123932)
XLA Ops:
  0.0 1.3 %shard_map.64 = (f32[2,4,2,8,512]{4,3,2,1,0:T(8,128)S(1)}, f32[2,4,2,8,512]{4,3,2,1,0:T(8,128)S(1)}, f32[8,2,8,512]{3,2,1,0:T(8,128)S(1)}) custom-call(s32[1,128]{1,0:T(1,128)} %bitcast.7, f32[2,8,2,8,512]{4,3,2,1,0:T(8,128)} %bitcast.4, f32[2,8,2,8,512]{4,3,2,1,0:T(8,128)} %bitcast.6), custom_call_target="tpu_custom_call" | custom-call | tf_op jit(solution)/shard_map/pallas_call | solution.py:296
  1.4 1.8 %shard_map.65 = f32[16,2,8,512]{3,2,1,0:T(8,128)} custom-call(f32[2,8,2,8,512]{4,3,2,1,0:T(8,128)} %bitcast.5, f32[8,2,8,512]{3,2,1,0:T(8,128)S(1)} %get-tuple-element.28.second), custom_call_target="tpu_custom_call" | custom-call | tf_op jit(solution)/shard_map/pallas_call | solution.py:328
  3.2 0.0 copy-start.2
  3.2 7.4 %all-to-all-start = ((f32[16,2,8,512]{3,2,1,0:T(8,128)}), f32[16,2,8,512]{3,2,1,0:T(8,128)S(1)}, u32[]{:S(2)}, u32[]{:S(2)}) async-start(f32[16,2,8,512]{3,2,1,0:T(8,128)} %shard_map.65), calls=%async_computation | async-start | bytes 1048576 | tf_op jit(solution)/shard_map/all_to_all | solution.py:341
  10.6 0.4 collective-permute-start.4
  11.0 1.3 %collective-permute-done.4.got = f32[2,4,2,8,512]{4,3,2,1,0:T(8,128)S(1)} collective-permute-done((f32[2,4,2,8,512]{4,3,2,1,0:T(8,128)S(1)}, f32[2,4,2,8,512]{4,3,2,1,0:T(8,128)S(1)}, u32[]{:S(2)}, u32[]{:S(2)}) %collective-permute-start.4) | collective-permute-done | bytes 262176 | tf_op jit(solution)/shard_map/ppermute | solution.py:327
  12.3 0.0 copy-start
  12.3 0.0 copy-start.1
  12.3 1.8 %collective-permute-start.5 = (f32[2,2,8,512]{3,2,1,0:T(8,128)S(1)}, f32[2,2,8,512]{3,2,1,0:T(8,128)S(1)}, u32[]{:S(2)}, u32[]{:S(2)}) collective-permute-start(f32[2,2,8,512]{3,2,1,0:T(8,128)S(1)} %get-tuple-element.38), channel_id=1, source_target_pairs={{0,2},{1,3},{2,0},{3,1},{4,6},{5,7},{6,4},{7,5},{16,18},{17,19},{1... | collective-permute-start | bytes 196616 | tf_op jit(solution)/shard_map/ppermute | solution.py:340
  14.2 2.4 %collective-permute-start.6 = (f32[2,2,8,512]{3,2,1,0:T(8,128)S(1)}, f32[2,2,8,512]{3,2,1,0:T(8,128)S(1)}, u32[]{:S(2)}, u32[]{:S(2)}) collective-permute-start(f32[2,2,8,512]{3,2,1,0:T(8,128)S(1)} %get-tuple-element.39), channel_id=1, source_target_pairs={{0,4},{1,5},{2,6},{3,7},{4,0},{5,1},{6,2},{7,3},{16,20},{17,21},{1... | collective-permute-start | bytes 196616 | tf_op jit(solution)/shard_map/ppermute | solution.py:340
  16.5 0.3 collective-permute-start.7
  16.8 1.8 %collective-permute-start.8 = (f32[2,2,8,512]{3,2,1,0:T(8,128)S(1)}, f32[2,2,8,512]{3,2,1,0:T(8,128)S(1)}, u32[]{:S(2)}, u32[]{:S(2)}) collective-permute-start(f32[2,2,8,512]{3,2,1,0:T(8,128)S(1)} %get-tuple-element.41), channel_id=1, source_target_pairs={{0,16},{1,17},{2,18},{3,19},{4,20},{5,21},{6,22},{7,23},{16,0},{17... | collective-permute-start | bytes 196616 | tf_op jit(solution)/shard_map/ppermute | solution.py:340
  18.6 0.6 collective-permute-start.9
  19.1 3.0 %collective-permute-done.5.refs_1_ = f32[2,2,8,512]{3,2,1,0:T(8,128)S(1)} collective-permute-done((f32[2,2,8,512]{3,2,1,0:T(8,128)S(1)}, f32[2,2,8,512]{3,2,1,0:T(8,128)S(1)}, u32[]{:S(2)}, u32[]{:S(2)}) %collective-permute-start.5) | collective-permute-done | bytes 65568 | tf_op jit(solution)/shard_map/ppermute | solution.py:340
  22.2 5.2 %collective-permute-start.10 = (f32[2,2,8,512]{3,2,1,0:T(8,128)S(1)}, f32[2,2,8,512]{3,2,1,0:T(8,128)S(1)}, u32[]{:S(2)}, u32[]{:S(2)}) collective-permute-start(f32[2,2,8,512]{3,2,1,0:T(8,128)S(1)} %get-tuple-element.43), channel_id=1, source_target_pairs={{0,20},{1,21},{2,22},{3,23},{4,16},{5,17},{6,18},{7,19},{16,4},{17... | collective-permute-start | bytes 196616 | tf_op jit(solution)/shard_map/ppermute | solution.py:340
  27.4 4.7 %collective-permute-done.6.refs_2_ = f32[2,2,8,512]{3,2,1,0:T(8,128)S(1)} collective-permute-done((f32[2,2,8,512]{3,2,1,0:T(8,128)S(1)}, f32[2,2,8,512]{3,2,1,0:T(8,128)S(1)}, u32[]{:S(2)}, u32[]{:S(2)}) %collective-permute-start.6) | collective-permute-done | bytes 65568 | tf_op jit(solution)/shard_map/ppermute | solution.py:340
  32.0 1.8 %collective-permute-start.11 = (f32[2,2,8,512]{3,2,1,0:T(8,128)S(1)}, f32[2,2,8,512]{3,2,1,0:T(8,128)S(1)}, u32[]{:S(2)}, u32[]{:S(2)}) collective-permute-start(f32[2,2,8,512]{3,2,1,0:T(8,128)S(1)} %get-tuple-element.44), channel_id=1, source_target_pairs={{0,22},{1,23},{2,20},{3,21},{4,18},{5,19},{6,16},{7,17},{16,6},{17... | collective-permute-start | bytes 196616 | tf_op jit(solution)/shard_map/ppermute | solution.py:340
  33.9 0.0 collective-permute-done.7.refs_3_
  33.9 0.0 collective-permute-done.8.refs_4_
  33.9 0.0 collective-permute-done.9.refs_5_
  33.9 2.6 %collective-permute-done.10.refs_6_ = f32[2,2,8,512]{3,2,1,0:T(8,128)S(1)} collective-permute-done((f32[2,2,8,512]{3,2,1,0:T(8,128)S(1)}, f32[2,2,8,512]{3,2,1,0:T(8,128)S(1)}, u32[]{:S(2)}, u32[]{:S(2)}) %collective-permute-start.10) | collective-permute-done | bytes 65568 | tf_op jit(solution)/shard_map/ppermute | solution.py:340
  36.4 2.5 %collective-permute-done.11.refs_7_ = f32[2,2,8,512]{3,2,1,0:T(8,128)S(1)} collective-permute-done((f32[2,2,8,512]{3,2,1,0:T(8,128)S(1)}, f32[2,2,8,512]{3,2,1,0:T(8,128)S(1)}, u32[]{:S(2)}, u32[]{:S(2)}) %collective-permute-start.11) | collective-permute-done | bytes 65568 | tf_op jit(solution)/shard_map/ppermute | solution.py:340
  39.0 0.0 copy-done.2
  39.0 0.0 copy-done
  39.0 0.0 copy-done.1
  39.0 1.1 %shard_map.69 = (f32[4,2,8,512]{3,2,1,0:T(8,128)S(1)}, f32[4,2,8,512]{3,2,1,0:T(8,128)S(1)}) custom-call(f32[2,2,8,512]{3,2,1,0:T(8,128)S(1)} %get-tuple-element.37.refs_0_, f32[2,2,8,512]{3,2,1,0:T(8,128)S(1)} %collective-permute-done.5.refs_1_, f32[2,2,8,512]{3,2,1,0:T(8,128)S(1)} %collective-permute-done.6.refs_2_, ...), custom_call_target="tpu_custom_call" | custom-call | flops 301989888 | bytes 4194304 | tf_op jit(solution)/shard_map/pallas_call | solution.py:363
  40.1 0.1 collective-permute-start.12
  40.2 0.0 all-to-all-done.got
  40.2 1.1 %shard_map.66 = (f32[4,2,8,512]{3,2,1,0:T(8,128)S(1)}, f32[4,2,8,512]{3,2,1,0:T(8,128)S(1)}) custom-call(f32[16,2,8,512]{3,2,1,0:T(8,128)S(1)} %all-to-all-done.got, bf16[2,256,256]{2,1,0:T(8,128)(2,1)S(1)} %copy-done.1, bf16[2,256,256]{2,1,0:T(8,128)(2,1)S(1)} %copy-done, f32[2,32,128]{2,1,0:T(8,128)S(1)} %copy-done.2), custom_call_target="tpu_custom_call" | custom-call | flops 301989888 | bytes 4194304 | tf_op jit(solution)/shard_map/pallas_call | solution.py:375
  41.3 0.6 collective-permute-start
  41.9 0.0 collective-permute-done.12.got
  41.9 0.1 collective-permute-start.13
  42.0 0.6 %collective-permute-start.14 = (f32[2,2,8,512]{3,2,1,0:T(8,128)S(1)}, f32[2,2,8,512]{3,2,1,0:T(8,128)S(1)}, u32[]{:S(2)}, u32[]{:S(2)}) collective-permute-start(f32[2,2,8,512]{3,2,1,0:T(8,128)S(1)} %get-tuple-element.49), channel_id=1, source_target_pairs={{0,4},{1,5},{2,6},{3,7},{4,0},{5,1},{6,2},{7,3},{8,12},{9,13},{10,... | collective-permute-start | bytes 196616 | tf_op jit(solution)/shard_map/ppermute | solution.py:389
  42.6 3.7 %collective-permute-start.15 = (f32[2,2,8,512]{3,2,1,0:T(8,128)S(1)}, f32[2,2,8,512]{3,2,1,0:T(8,128)S(1)}, u32[]{:S(2)}, u32[]{:S(2)}) collective-permute-start(f32[2,2,8,512]{3,2,1,0:T(8,128)S(1)} %get-tuple-element.50), channel_id=1, source_target_pairs={{0,6},{1,7},{2,4},{3,5},{4,2},{5,3},{6,0},{7,1},{8,14},{9,15},{10,... | collective-permute-start | bytes 196616 | tf_op jit(solution)/shard_map/ppermute | solution.py:389
  46.3 0.0 collective-permute-done.got
  46.4 0.1 collective-permute-start.1
  46.4 0.6 %collective-permute-start.2 = (f32[2,2,8,512]{3,2,1,0:T(8,128)S(1)}, f32[2,2,8,512]{3,2,1,0:T(8,128)S(1)}, u32[]{:S(2)}, u32[]{:S(2)}) collective-permute-start(f32[2,2,8,512]{3,2,1,0:T(8,128)S(1)} %get-tuple-element.33), channel_id=1, source_target_pairs={{0,4},{1,5},{2,6},{3,7},{4,0},{5,1},{6,2},{7,3},{8,12},{9,13},{10,... | collective-permute-start | bytes 196616 | tf_op jit(solution)/shard_map/ppermute | solution.py:389
  47.1 0.0 collective-permute-done.13.refs_1_
  47.1 3.7 %collective-permute-start.3 = (f32[2,2,8,512]{3,2,1,0:T(8,128)S(1)}, f32[2,2,8,512]{3,2,1,0:T(8,128)S(1)}, u32[]{:S(2)}, u32[]{:S(2)}) collective-permute-start(f32[2,2,8,512]{3,2,1,0:T(8,128)S(1)} %get-tuple-element.34), channel_id=1, source_target_pairs={{0,6},{1,7},{2,4},{3,5},{4,2},{5,3},{6,0},{7,1},{8,14},{9,15},{10,... | collective-permute-start | bytes 196616 | tf_op jit(solution)/shard_map/ppermute | solution.py:389
  50.8 0.3 collective-permute-done.14.refs_2_
  51.1 0.0 collective-permute-done.15.refs_3_
  51.1 0.8 %shard_map.72.refs_4_ = f32[2,8,2,8,512]{4,3,2,1,0:T(8,128)} custom-call(f32[2,2,8,512]{3,2,1,0:T(8,128)S(1)} %shard_map.71.refs_0_, f32[2,2,8,512]{3,2,1,0:T(8,128)S(1)} %collective-permute-done.13.refs_1_, f32[2,2,8,512]{3,2,1,0:T(8,128)S(1)} %collective-permute-done.14.refs_2_, f32[2,2,8,512]{3,2,1,0:T(8,128)S(1)} %collective-permute-done.15.refs_3_), custom_call_target="tpu_custom_call" | custom-call | tf_op jit(solution)/shard_map/pallas_call | solution.py:399
  51.9 0.0 collective-permute-done.1.refs_1_
  51.9 4.2 %collective-permute-done.2.refs_2_ = f32[2,2,8,512]{3,2,1,0:T(8,128)S(1)} collective-permute-done((f32[2,2,8,512]{3,2,1,0:T(8,128)S(1)}, f32[2,2,8,512]{3,2,1,0:T(8,128)S(1)}, u32[]{:S(2)}, u32[]{:S(2)}) %collective-permute-start.2) | collective-permute-done | bytes 65568 | tf_op jit(solution)/shard_map/ppermute | solution.py:389
  56.1 0.0 collective-permute-done.3.refs_3_
  56.1 0.8 %shard_map.73 = f32[2,8,2,8,512]{4,3,2,1,0:T(8,128)} custom-call(f32[2,2,8,512]{3,2,1,0:T(8,128)S(1)} %get-tuple-element.31.refs_0_, f32[2,2,8,512]{3,2,1,0:T(8,128)S(1)} %collective-permute-done.1.refs_1_, f32[2,2,8,512]{3,2,1,0:T(8,128)S(1)} %collective-permute-done.2.refs_2_, ...), custom_call_target="tpu_custom_call", output_to_operand_aliasing={{}: (4, {})} | custom-call | tf_op jit(solution)/shard_map/pallas_call | solution.py:399
  (4 shorter events, 0.1 us)
Async XLA Ops:
  3.2 35.8 %copy-start.2 = (f32[2,32,128]{2,1,0:T(8,128)S(1)}, f32[2,32,128]{2,1,0:T(8,128)}, u32[]{:S(2)}) copy-start(f32[2,32,128]{2,1,0:T(8,128)} %constant.8.clone.twist.refs_10_) | copy-start | bytes 98308
  3.2 37.0 %all-to-all-start = ((f32[16,2,8,512]{3,2,1,0:T(8,128)}), f32[16,2,8,512]{3,2,1,0:T(8,128)S(1)}, u32[]{:S(2)}, u32[]{:S(2)}) async-start(f32[16,2,8,512]{3,2,1,0:T(8,128)} %shard_map.65), calls=%async_computation | async-start | bytes 1048576 | tf_op jit(solution)/shard_map/all_to_all | solution.py:341
  10.6 1.7 %collective-permute-start.4 = (f32[2,4,2,8,512]{4,3,2,1,0:T(8,128)S(1)}, f32[2,4,2,8,512]{4,3,2,1,0:T(8,128)S(1)}, u32[]{:S(2)}, u32[]{:S(2)}) collective-permute-start(f32[2,4,2,8,512]{4,3,2,1,0:T(8,128)S(1)} %get-tuple-element.36), channel_id=1, source_target_pairs={{0,1},{1,0},{2,3},{3,2},{4,5},{5,4},{6,7},{7,6},{8,9},{9,8},{10,11... | collective-permute-start | bytes 786440 | tf_op jit(solution)/shard_map/ppermute | solution.py:327
  12.3 26.7 %copy-start = (bf16[2,256,256]{2,1,0:T(8,128)(2,1)S(1)}, bf16[2,256,256]{2,1,0:T(8,128)(2,1)}, u32[]{:S(2)}) copy-start(bf16[2,256,256]{2,1,0:T(8,128)(2,1)} %constant.7.clone.backward.refs_9_) | copy-start | bytes 786436
  12.3 26.7 %copy-start.1 = (bf16[2,256,256]{2,1,0:T(8,128)(2,1)S(1)}, bf16[2,256,256]{2,1,0:T(8,128)(2,1)}, u32[]{:S(2)}) copy-start(bf16[2,256,256]{2,1,0:T(8,128)(2,1)} %constant.6.clone.forward.refs_8_) | copy-start | bytes 786436
  12.3 9.8 %collective-permute-start.5 = (f32[2,2,8,512]{3,2,1,0:T(8,128)S(1)}, f32[2,2,8,512]{3,2,1,0:T(8,128)S(1)}, u32[]{:S(2)}, u32[]{:S(2)}) collective-permute-start(f32[2,2,8,512]{3,2,1,0:T(8,128)S(1)} %get-tuple-element.38), channel_id=1, source_target_pairs={{0,2},{1,3},{2,0},{3,1},{4,6},{5,7},{6,4},{7,5},{16,18},{17,19},{1... | collective-permute-start | bytes 196616 | tf_op jit(solution)/shard_map/ppermute | solution.py:340
  14.2 17.8 %collective-permute-start.6 = (f32[2,2,8,512]{3,2,1,0:T(8,128)S(1)}, f32[2,2,8,512]{3,2,1,0:T(8,128)S(1)}, u32[]{:S(2)}, u32[]{:S(2)}) collective-permute-start(f32[2,2,8,512]{3,2,1,0:T(8,128)S(1)} %get-tuple-element.39), channel_id=1, source_target_pairs={{0,4},{1,5},{2,6},{3,7},{4,0},{5,1},{6,2},{7,3},{16,20},{17,21},{1... | collective-permute-start | bytes 196616 | tf_op jit(solution)/shard_map/ppermute | solution.py:340
  16.5 17.3 %collective-permute-start.7 = (f32[2,2,8,512]{3,2,1,0:T(8,128)S(1)}, f32[2,2,8,512]{3,2,1,0:T(8,128)S(1)}, u32[]{:S(2)}, u32[]{:S(2)}) collective-permute-start(f32[2,2,8,512]{3,2,1,0:T(8,128)S(1)} %get-tuple-element.40), channel_id=1, source_target_pairs={{0,6},{1,7},{2,4},{3,5},{4,2},{5,3},{6,0},{7,1},{16,22},{17,23},{1... | collective-permute-start | bytes 196616 | tf_op jit(solution)/shard_map/ppermute | solution.py:340
  16.8 17.1 %collective-permute-start.8 = (f32[2,2,8,512]{3,2,1,0:T(8,128)S(1)}, f32[2,2,8,512]{3,2,1,0:T(8,128)S(1)}, u32[]{:S(2)}, u32[]{:S(2)}) collective-permute-start(f32[2,2,8,512]{3,2,1,0:T(8,128)S(1)} %get-tuple-element.41), channel_id=1, source_target_pairs={{0,16},{1,17},{2,18},{3,19},{4,20},{5,21},{6,22},{7,23},{16,0},{17... | collective-permute-start | bytes 196616 | tf_op jit(solution)/shard_map/ppermute | solution.py:340
  18.6 15.3 %collective-permute-start.9 = (f32[2,2,8,512]{3,2,1,0:T(8,128)S(1)}, f32[2,2,8,512]{3,2,1,0:T(8,128)S(1)}, u32[]{:S(2)}, u32[]{:S(2)}) collective-permute-start(f32[2,2,8,512]{3,2,1,0:T(8,128)S(1)} %get-tuple-element.42), channel_id=1, source_target_pairs={{0,18},{1,19},{2,16},{3,17},{4,22},{5,23},{6,20},{7,21},{16,2},{17... | collective-permute-start | bytes 196616 | tf_op jit(solution)/shard_map/ppermute | solution.py:340
  22.2 14.3 %collective-permute-start.10 = (f32[2,2,8,512]{3,2,1,0:T(8,128)S(1)}, f32[2,2,8,512]{3,2,1,0:T(8,128)S(1)}, u32[]{:S(2)}, u32[]{:S(2)}) collective-permute-start(f32[2,2,8,512]{3,2,1,0:T(8,128)S(1)} %get-tuple-element.43), channel_id=1, source_target_pairs={{0,20},{1,21},{2,22},{3,23},{4,16},{5,17},{6,18},{7,19},{16,4},{17... | collective-permute-start | bytes 196616 | tf_op jit(solution)/shard_map/ppermute | solution.py:340
  32.0 7.0 %collective-permute-start.11 = (f32[2,2,8,512]{3,2,1,0:T(8,128)S(1)}, f32[2,2,8,512]{3,2,1,0:T(8,128)S(1)}, u32[]{:S(2)}, u32[]{:S(2)}) collective-permute-start(f32[2,2,8,512]{3,2,1,0:T(8,128)S(1)} %get-tuple-element.44), channel_id=1, source_target_pairs={{0,22},{1,23},{2,20},{3,21},{4,18},{5,19},{6,16},{7,17},{16,6},{17... | collective-permute-start | bytes 196616 | tf_op jit(solution)/shard_map/ppermute | solution.py:340
  40.1 1.7 %collective-permute-start.12 = (f32[4,2,8,512]{3,2,1,0:T(8,128)S(1)}, f32[4,2,8,512]{3,2,1,0:T(8,128)S(1)}, u32[]{:S(2)}, u32[]{:S(2)}) collective-permute-start(f32[4,2,8,512]{3,2,1,0:T(8,128)S(1)} %get-tuple-element.46), channel_id=1, source_target_pairs={{0,1},{1,0},{2,3},{3,2},{4,5},{5,4},{6,7},{7,6},{8,9},{9,8},{10,11... | collective-permute-start | bytes 393224 | tf_op jit(solution)/shard_map/ppermute | solution.py:385
  41.3 5.0 %collective-permute-start = (f32[4,2,8,512]{3,2,1,0:T(8,128)S(1)}, f32[4,2,8,512]{3,2,1,0:T(8,128)S(1)}, u32[]{:S(2)}, u32[]{:S(2)}) collective-permute-start(f32[4,2,8,512]{3,2,1,0:T(8,128)S(1)} %get-tuple-element.30), channel_id=1, source_target_pairs={{0,1},{1,0},{2,3},{3,2},{4,5},{5,4},{6,7},{7,6},{8,9},{9,8},{10,11... | collective-permute-start | bytes 393224 | tf_op jit(solution)/shard_map/ppermute | solution.py:385
  41.9 5.2 %collective-permute-start.13 = (f32[2,2,8,512]{3,2,1,0:T(8,128)S(1)}, f32[2,2,8,512]{3,2,1,0:T(8,128)S(1)}, u32[]{:S(2)}, u32[]{:S(2)}) collective-permute-start(f32[2,2,8,512]{3,2,1,0:T(8,128)S(1)} %get-tuple-element.48), channel_id=1, source_target_pairs={{0,2},{1,3},{2,0},{3,1},{4,6},{5,7},{6,4},{7,5},{8,10},{9,11},{10,... | collective-permute-start | bytes 196616 | tf_op jit(solution)/shard_map/ppermute | solution.py:389
  42.0 9.2 %collective-permute-start.14 = (f32[2,2,8,512]{3,2,1,0:T(8,128)S(1)}, f32[2,2,8,512]{3,2,1,0:T(8,128)S(1)}, u32[]{:S(2)}, u32[]{:S(2)}) collective-permute-start(f32[2,2,8,512]{3,2,1,0:T(8,128)S(1)} %get-tuple-element.49), channel_id=1, source_target_pairs={{0,4},{1,5},{2,6},{3,7},{4,0},{5,1},{6,2},{7,3},{8,12},{9,13},{10,... | collective-permute-start | bytes 196616 | tf_op jit(solution)/shard_map/ppermute | solution.py:389
  42.6 8.5 %collective-permute-start.15 = (f32[2,2,8,512]{3,2,1,0:T(8,128)S(1)}, f32[2,2,8,512]{3,2,1,0:T(8,128)S(1)}, u32[]{:S(2)}, u32[]{:S(2)}) collective-permute-start(f32[2,2,8,512]{3,2,1,0:T(8,128)S(1)} %get-tuple-element.50), channel_id=1, source_target_pairs={{0,6},{1,7},{2,4},{3,5},{4,2},{5,3},{6,0},{7,1},{8,14},{9,15},{10,... | collective-permute-start | bytes 196616 | tf_op jit(solution)/shard_map/ppermute | solution.py:389
  46.4 5.5 %collective-permute-start.1 = (f32[2,2,8,512]{3,2,1,0:T(8,128)S(1)}, f32[2,2,8,512]{3,2,1,0:T(8,128)S(1)}, u32[]{:S(2)}, u32[]{:S(2)}) collective-permute-start(f32[2,2,8,512]{3,2,1,0:T(8,128)S(1)} %get-tuple-element.32), channel_id=1, source_target_pairs={{0,2},{1,3},{2,0},{3,1},{4,6},{5,7},{6,4},{7,5},{8,10},{9,11},{10,... | collective-permute-start | bytes 196616 | tf_op jit(solution)/shard_map/ppermute | solution.py:389
  46.4 9.6 %collective-permute-start.2 = (f32[2,2,8,512]{3,2,1,0:T(8,128)S(1)}, f32[2,2,8,512]{3,2,1,0:T(8,128)S(1)}, u32[]{:S(2)}, u32[]{:S(2)}) collective-permute-start(f32[2,2,8,512]{3,2,1,0:T(8,128)S(1)} %get-tuple-element.33), channel_id=1, source_target_pairs={{0,4},{1,5},{2,6},{3,7},{4,0},{5,1},{6,2},{7,3},{8,12},{9,13},{10,... | collective-permute-start | bytes 196616 | tf_op jit(solution)/shard_map/ppermute | solution.py:389
  47.1 9.0 %collective-permute-start.3 = (f32[2,2,8,512]{3,2,1,0:T(8,128)S(1)}, f32[2,2,8,512]{3,2,1,0:T(8,128)S(1)}, u32[]{:S(2)}, u32[]{:S(2)}) collective-permute-start(f32[2,2,8,512]{3,2,1,0:T(8,128)S(1)} %get-tuple-element.34), channel_id=1, source_target_pairs={{0,6},{1,7},{2,4},{3,5},{4,2},{5,3},{6,0},{7,1},{8,14},{9,15},{10,... | collective-permute-start | bytes 196616 | tf_op jit(solution)/shard_map/ppermute | solution.py:389
